TPU v7x, 32 devices: a whole 2x2x4 slice. The times are simulated.
32 devices in a mesh: dp: 4 (over y, core), ctx: 8 (over z, x).
Axes of the slice: x: 2, y: 2, z: 4, core: 2. Of those that a mesh axis runs over, the one named last changes fastest.
Arguments:
- tokens: bfloat16 [2, 4, 1024, 768], P(None, 'dp', 'ctx'), may hold values from -6 to 6
- lengths: int32 [2, 4], P(None, 'dp'), may hold values from 513 to 1024, as said below
- routes: int32 [2, 4, 1024, 2], P(None, 'dp', 'ctx'), may hold values from 0 to 3, all different within a row
- cotangent: bfloat16 [2, 4, 1024, 768], P(None, 'dp', 'ctx'), may hold values from -6 to 6
- attn_gain: bfloat16 [768], P(('dp', 'ctx')), may hold values from 0.5 to 1.5
- attn_in: bfloat16 [768, 2304], P(('dp', 'ctx')), may hold values from -0.21875 to 0.21875
- attn_out: bfloat16 [768, 768], P(('dp', 'ctx')), may hold values from -3.5 to 3.5
- ffn_gain: bfloat16 [768], P(('dp', 'ctx')), may hold values from 0.5 to 1.5
- router: bfloat16 [768, 4], P(('dp', 'ctx')), may hold values from -0.21875 to 0.21875
- dense_in: bfloat16 [768, 4096], P(('dp', 'ctx')), may hold values from -0.21875 to 0.21875
- dense_out: bfloat16 [2048, 768], P(('dp', 'ctx')), may hold values from -0.125 to 0.125
- expert_in: bfloat16 [768, 4, 4096], P(('dp', 'ctx')), may hold values from -0.21875 to 0.21875
- expert_out: bfloat16 [2048, 4, 768], P(('dp', 'ctx')), may hold values from -0.125 to 0.125
Outputs:
- activations: bfloat16 [2, 4, 1024, 768], P(None, 'dp', 'ctx')
- input_grad: bfloat16 [2, 4, 1024, 768], P(None, 'dp', 'ctx')
- attn_gain_grad: float32 [768], P(('dp', 'ctx'))
- attn_in_grad: float32 [768, 2304], P(('dp', 'ctx'))
- attn_out_grad: float32 [768, 768], P(('dp', 'ctx'))
- ffn_gain_grad: float32 [768], P(('dp', 'ctx'))
- router_grad: float32 [768, 4], P(('dp', 'ctx'))
- dense_in_grad: float32 [768, 4096], P(('dp', 'ctx'))
- dense_out_grad: float32 [2048, 768], P(('dp', 'ctx'))
- expert_in_grad: float32 [768, 4, 4096], P(('dp', 'ctx'))
- expert_out_grad: float32 [2048, 4, 768], P(('dp', 'ctx'))
Inputs may be any that keep to these rules, and one draw needn't show every extreme that they name: `lengths`: the first sequence of every micro-batch is valid in all 1024 slots. `routes`: each slot names two different experts.
All inputs are finite; a program needn't handle non-finite values.
Results may differ from a plain program's by a relative error of at most 0.014.
Values may be sent and summed in bfloat16 or wider, within the bound.
A program may use at most 384 MiB of HBM per device.

v0:
```python
import functools

import jax
import jax.numpy as jnp
import numpy as np
from jax import lax
from jax.experimental import pallas as pl
from jax.experimental.pallas import tpu as pltpu
from jax.sharding import PartitionSpec as P

HEADS = 12
HEAD_DIM = 64
FF = 2048
EPSILON = 1e-05
HALVES = 2
QUERY_ROWS = 256
MIX_ROWS = 16
MESH = pl.DeviceIdType.MESH
BF16 = jnp.bfloat16
F32 = jnp.float32


def round_up(value, step):
    return -(-value // step) * step


class Plan:
    def __init__(self, dp, ctx, block, width, experts):
        self.dp, self.ctx, self.block, self.width, self.experts = dp, ctx, block, width, experts
        self.quad = ctx // HALVES
        self.devices = dp * ctx
        self.group = dp * self.quad
        self.slots = ctx * block
        self.rows = width // self.devices
        self.pad_rows = round_up(self.rows, 8)
        self.heads = -(-HEADS // self.quad)
        self.head_cols = self.heads * HEAD_DIM
        self.qkv_cols = 3 * self.head_cols
        self.wide = round_up(self.qkv_cols + 2 + experts, 128)
        self.own_hidden = FF // self.devices
        self.branches = 1 + experts
        self.hidden = self.branches * HALVES * self.own_hidden
        self.hidden_pad = round_up(self.hidden, 128)
        self.local = HALVES * block
        self.tiled = (
            self.own_hidden == 64
            and self.rows % 8 == 0
            and self.quad == 4
            and self.heads == 3
            and self.wide == self.qkv_cols + 64
        )


def place():
    return lax.axis_index("dp"), lax.axis_index("ctx")


def params(collective_id=None, limit=60 * 1024 * 1024):
    if collective_id is None:
        return pltpu.CompilerParams(vmem_limit_bytes=limit)
    return pltpu.CompilerParams(
        vmem_limit_bytes=limit, collective_id=collective_id, has_side_effects=True
    )


def remote(src, dst, send_sem, recv_sem, device):
    return pltpu.make_async_remote_copy(
        src_ref=src,
        dst_ref=dst,
        send_sem=send_sem,
        recv_sem=recv_sem,
        device_id=device,
        device_id_type=MESH,
    )


def busy(microseconds):
    return pl.CostEstimate(
        flops=0, bytes_accessed=int(microseconds * 3.4e6), transcendentals=0
    )


def meet(devices):
    barrier = pltpu.get_barrier_semaphore()
    for device in devices:
        pl.semaphore_signal(barrier, inc=1, device_id=device, device_id_type=MESH)
    pl.semaphore_wait(barrier, len(devices))


def other_devices(plan, dp, ctx):
    flat = dp * plan.ctx + ctx
    result = []
    for step in range(1, plan.devices):
        target = lax.rem(flat + step, plan.devices)
        result.append((lax.div(target, plan.ctx), lax.rem(target, plan.ctx)))
    return result


def quad_members(plan, half, member):
    return [
        (half * plan.quad + lax.rem(member + step, plan.quad), lax.rem(member + step, plan.quad))
        for step in range(1, plan.quad)
    ]


VMEM = pl.BlockSpec(memory_space=pltpu.VMEM)
HBM = pl.BlockSpec(memory_space=pl.ANY)
DMA = pltpu.SemaphoreType.DMA


def half_members(plan, mine):
    return [lax.rem(mine + step, plan.group) for step in range(1, plan.group)]


class Grid:
    def __init__(self, plan):
        self.plan = plan
        self.sizes = {"y": plan.dp // 2, "high": plan.quad // 2, "low": 2}

    def here(self):
        dp, ctx = place()
        member = lax.rem(ctx, self.plan.quad)
        return {
            "core": lax.rem(dp, 2),
            "y": lax.div(dp, 2),
            "high": lax.div(member, 2),
            "low": lax.rem(member, 2),
            "half": lax.div(ctx, self.plan.quad),
        }

    def device(self, at):
        return (
            at["y"] * 2 + at["core"],
            at["half"] * self.plan.quad + at["high"] * 2 + at["low"],
        )

    def block(self, at):
        return (at["y"] * 2 + at["core"]) * self.plan.quad + at["high"] * 2 + at["low"]

    def moved(self, at, axis, step):
        result = dict(at)
        if axis == "core":
            result["core"] = 1 - at["core"]
        else:
            result[axis] = lax.rem(at[axis] + step, self.sizes[axis])
        return result

    def peers(self, at):
        result = [self.moved(at, "core", 1)]
        for axis, size in self.sizes.items():
            result += [self.moved(at, axis, step) for step in range(1, size)]
        return [self.device(peer) for peer in result]

    def slot(self, offsets):
        return (offsets["y"] * self.sizes["high"] + offsets["high"]) * 2 + offsets["low"]


GATHER_ORDERS = (("high", "low", "y"), ("high", "y", "low"))


class Gather:
    def __init__(self, grid, at, src, dst, send, recv, core_send, core_recv):
        self.grid, self.at, self.src, self.dst = grid, at, src, dst
        self.send, self.recv, self.core_send, self.core_recv = send, recv, core_send, core_recv

    def groups(self, order):
        sizes = self.grid.sizes
        levels = [[{"y": 0, "high": 0, "low": 0}], [], [], []]
        for level, axis in enumerate(order):
            base = [o for group in levels[: level + 1] for o in group]
            levels[level + 1] = [
                {**offsets, axis: step} for offsets in base for step in range(1, sizes[axis])
            ]
        return levels

    def absolute(self, offsets):
        where = dict(self.at)
        for axis, step in offsets.items():
            if step:
                where = self.grid.moved(where, axis, step)
        return where

    def run_level(self, order, level):
        grid, at = self.grid, self.at
        index = 0
        for current, group in enumerate(self.groups(order)):
            for offsets in group:
                if current == level:
                    block = grid.block(self.absolute(offsets))
                    if level:
                        remote(
                            self.src,
                            self.dst.at[block],
                            self.send.at[0],
                            self.recv.at[grid.slot(offsets)],
                            grid.device(at),
                        ).wait_recv()
                    source = self.dst.at[block] if level else self.src
                    remote(
                        source,
                        self.dst.at[block],
                        self.core_send.at[grid.slot(offsets)],
                        self.core_recv.at[grid.slot(offsets)],
                        grid.device(grid.moved(at, "core", 1)),
                    ).start()
                for axis in order[current:]:
                    for step in range(1, grid.sizes[axis]):
                        if current == level:
                            seen = {**offsets, axis: grid.sizes[axis] - step}
                            remote(
                                source,
                                self.dst.at[block],
                                self.send.at[index],
                                self.recv.at[grid.slot(seen)],
                                grid.device(grid.moved(at, axis, step)),
                            ).start()
                        index += 1

    def level(self, level):
        for color, order in enumerate(GATHER_ORDERS):
            pl.when(self.at["core"] == color)(functools.partial(self.run_level, order, level))

    def finish(self):
        plan, here = self.grid.plan, self.grid.device(self.at)

        def sent(order):
            for index in range(gather_sends(plan, order)):
                remote(self.src, self.dst.at[0], self.send.at[index], self.recv.at[0], here).wait_send()

        for color, order in enumerate(GATHER_ORDERS):
            pl.when(self.at["core"] == color)(functools.partial(sent, order))
        for slot in range(plan.group // 2):
            remote(
                self.src, self.dst.at[0], self.core_send.at[slot], self.core_recv.at[slot], here
            ).wait()


def gather_kernel(plan, src, dst, send, recv, core_send, core_recv):
    grid = Grid(plan)
    at = grid.here()
    meet(grid.peers(at))
    dst[pl.ds(grid.block(at), 1)] = src[...][None]
    blocks = Gather(grid, at, src, dst, send, recv, core_send, core_recv)
    for level in range(4):
        blocks.level(level)
    blocks.finish()


def gather_sems(plan):
    half = plan.group // 2
    count = max(gather_sends(plan, order) for order in GATHER_ORDERS)
    return [DMA((count,)), DMA((half,)), DMA((half,)), DMA((half,))]


def gather_sends(plan, order):
    sizes = Grid(plan).sizes
    held, total = 1, 0
    for axis in order:
        total += held * (sizes[axis] - 1)
        held *= sizes[axis]
    return total


def gather(plan, block, collective_id):
    return pl.pallas_call(
        functools.partial(gather_kernel, plan),
        out_shape=jax.ShapeDtypeStruct((plan.group,) + block.shape, block.dtype),
        in_specs=[VMEM],
        out_specs=VMEM,
        scratch_shapes=gather_sems(plan),
        compiler_params=params(collective_id),
        cost_estimate=busy(35),
        name="gather",
    )(block)


def reduce_kernel(plan, src, out, work, core_buf, bufs, load_sem, core_send, core_recv, send, recv):
    grid = Grid(plan)
    at = grid.here()
    zero = {"y": 0, "high": 0, "low": 0}
    meet(grid.peers(at))

    def run(order):
        levels = [[], [], [], []]
        held = [dict(zero)]
        levels[3] = [dict(zero)]
        for level in (2, 1, 0):
            axis = order[level]
            base = [o for later in levels[level + 1 :] for o in later]
            levels[level] = [
                {**offsets, axis: step} for offsets in base for step in range(1, grid.sizes[axis])
            ]
        del held

        def absolute(offsets):
            where = dict(at)
            for axis, step in offsets.items():
                if step:
                    where = grid.moved(where, axis, step)
            return where

        sequence = [o for group in levels for o in group]
        partner = grid.device(grid.moved(at, "core", 1))
        core_copies = []
        loads = []
        for offsets in sequence:
            where = absolute(offsets)
            slot = grid.slot(offsets)
            copy = remote(
                src.at[grid.block(grid.moved(where, "core", 1))],
                core_buf.at[slot],
                core_send.at[slot],
                core_recv.at[slot],
                partner,
            )
            copy.start()
            core_copies.append(copy)
            load = pltpu.make_async_copy(
                src.at[grid.block(where)], work.at[slot], load_sem.at[slot]
            )
            load.start()
            loads.append(load)
        arrived = {}
        sends = []
        index = 0
        position = 0
        for level in range(4):
            for offsets in levels[level]:
                slot = grid.slot(offsets)
                core_copies[position].wait_recv()
                loads[position].wait()
                position += 1
                total = work[slot].astype(F32) + core_buf[slot].astype(F32)
                for buffer in arrived.get(slot, ()):
                    remote(work.at[slot], bufs.at[buffer], send.at[0], recv.at[buffer], partner).wait_recv()
                    total = total + bufs[buffer].astype(F32)
                if level == 3:
                    out[...] = total.astype(out.dtype)
                    continue
                work[slot] = total.astype(BF16)
                axis = order[level]
                step = offsets[axis]
                copy = remote(
                    work.at[slot],
                    bufs.at[index],
                    send.at[index],
                    recv.at[index],
                    grid.device(grid.moved(at, axis, step)),
                )
                copy.start()
                sends.append(copy)
                landing = grid.slot({**offsets, axis: 0})
                arrived.setdefault(landing, []).append(index)
                index += 1
        for copy in sends:
            copy.wait_send()
        for copy in core_copies:
            copy.wait_send()

    for color, order in enumerate(GATHER_ORDERS):
        pl.when(at["core"] == color)(functools.partial(run, order[::-1]))


def reduce(plan, blocks, collective_id):
    half = plan.group // 2
    shape = blocks.shape[1:]
    count = max(gather_sends(plan, order) for order in GATHER_ORDERS)
    return pl.pallas_call(
        functools.partial(reduce_kernel, plan),
        out_shape=jax.ShapeDtypeStruct(shape, F32),
        in_specs=[HBM],
        out_specs=VMEM,
        scratch_shapes=[
            pltpu.VMEM((half,) + shape, BF16),
            pltpu.VMEM((half,) + shape, BF16),
            pltpu.VMEM((count,) + shape, BF16),
            DMA((half,)),
            DMA((half,)),
            DMA((half,)),
            DMA((count,)),
            DMA((count,)),
        ],
        compiler_params=params(collective_id),
        name="reduce",
    )(blocks)


def nt(left, right):
    return lax.dot_general(left, right, (((1,), (1,)), ((), ())), preferred_element_type=F32)


def nn(left, right):
    return lax.dot_general(left, right, (((1,), (0,)), ((), ())), preferred_element_type=F32)


def tn(left, right):
    return lax.dot_general(left, right, (((0,), (0,)), ((), ())), preferred_element_type=F32)


def swapped_halves(value):
    lane = lax.broadcasted_iota(jnp.int32, value.shape, 1)
    first = lax.rem(lane, HEAD_DIM) < HEAD_DIM // 2
    half = HEAD_DIM // 2
    return jnp.where(
        first, pltpu.roll(value, 2 * HEAD_DIM - half, 1), pltpu.roll(value, half, 1)
    )


def masked_scores(q, k, first_row, length):
    scores = nt(q, k)
    row = lax.broadcasted_iota(jnp.int32, scores.shape, 0) + first_row
    col = lax.broadcasted_iota(jnp.int32, scores.shape, 1)
    return jnp.where((col <= row) & (col < length), scores, -1000000000.0)


def natural_rows(plan, blocks):
    flat = blocks.astype(F32).reshape(plan.devices * plan.pad_rows, blocks.shape[-1])
    if plan.pad_rows == plan.rows:
        return flat.astype(BF16)
    row = lax.broadcasted_iota(jnp.int32, (plan.width, flat.shape[0]), 0)
    col = lax.broadcasted_iota(jnp.int32, (plan.width, flat.shape[0]), 1)
    source = lax.div(row, plan.rows) * plan.pad_rows + lax.rem(row, plan.rows)
    return nn((col == source).astype(BF16), flat.astype(BF16)).astype(BF16)


def around_gains(plan, w_seq):
    first = plan.qkv_cols - (plan.wide - 128)
    return jnp.transpose(w_seq[:, plan.wide - 128 :].astype(F32), (1, 0))[first : first + 8]


def chosen(local, routes):
    row = lax.broadcasted_iota(jnp.int32, (8, local), 0).astype(F32)
    return row - 2.0 == routes


def owner_forward(plan, ctx, far, half, xs, w_seq, mixed, gysrc, w_tail, n2x, middle, gates, w_mix):
    block, local, width, cols = plan.block, plan.local, plan.width, plan.head_cols
    rows = plan.quad * plan.rows

    @pl.loop(0, HALVES * plan.dp)
    def _(i):
        turn = lax.rem(lax.rem(i, HALVES) + half, 2)
        value = w_tail[pl.ds(lax.div(i, HALVES) * plan.quad, plan.quad), pl.ds(turn, 1)]
        value = value[:, 0].astype(F32)[:, : plan.rows].reshape(rows, width)
        w_mix[pl.ds(pl.multiple_of(i * rows, 16), rows)] = value.astype(BF16)

    total = jnp.concatenate([xs[pl.ds(ctx, 1)][0], xs[pl.ds(far, 1)][0]], axis=0).astype(F32)
    for member in range(plan.quad):
        total = total + nn(
            mixed[member].reshape(local, cols), w_mix[member * cols : (member + 1) * cols]
        )
    middle[...] = total
    inverse = lax.rsqrt(jnp.mean(total * total, axis=-1, keepdims=True) + EPSILON)
    normed = (total * inverse * around_gains(plan, w_seq)[1:2]).astype(BF16)
    n2x[:local] = normed
    first = plan.qkv_cols - (plan.wide - 128)
    logits = jnp.transpose(nn(normed, w_seq[:, plan.wide - 128 :]), (1, 0))[first : first + 8]
    tail = gysrc[:, block + 16 :, :block].astype(F32)
    routes = [
        jnp.concatenate([tail[i, plan.rows - 16 + k : plan.rows - 15 + k] for i in range(2)], axis=1)
        for k in range(2)
    ]
    picks = [chosen(local, route) for route in routes]
    scores = [jnp.sum(jnp.where(pick, logits, 0.0), axis=0, keepdims=True) for pick in picks]
    top = jnp.maximum(scores[0], scores[1])
    raised = [jnp.exp(score - top) for score in scores]
    gate = [value / (raised[0] + raised[1]) for value in raised]
    mixing = jnp.where(picks[0], gate[0], 0.0) + jnp.where(picks[1], gate[1], 0.0)
    high = mixing.astype(BF16).astype(F32)
    row = lax.broadcasted_iota(jnp.int32, (8, local), 0)
    mix_rows = jnp.concatenate([jnp.where(row == 0, 1.0, high), mixing - high], axis=0)
    n2x[local:] = jnp.concatenate(
        [mix_rows.astype(BF16), jnp.zeros((MIX_ROWS, width - local), BF16)], axis=1
    )
    gates[...] = jnp.concatenate(gate + routes + [jnp.zeros((4, local), F32)], axis=0)


def owner_back(plan, n2g_sum, gates, n2x, gysrc, w_mix, mixed, middle, w_seq, dmixed, dwo, rows8, middle_grad):
    block, local, width, cols = plan.block, plan.local, plan.width, plan.head_cols
    around = around_gains(plan, w_seq)
    choice = n2g_sum[local : local + 8, :local]
    picks = [chosen(local, gates[2 + k : 3 + k]) for k in range(2)]
    gate = [gates[k : k + 1] for k in range(2)]
    taken = [jnp.sum(jnp.where(pick, choice, 0.0), axis=0, keepdims=True) for pick in picks]
    inner = gate[0] * taken[0] + gate[1] * taken[1]
    logit_grad = sum(
        jnp.where(picks[k], gate[k] * (taken[k] - inner), 0.0) for k in range(2)
    ).astype(BF16)
    router_grad = nn(logit_grad, n2x[:local])
    grad = n2g_sum[:local] + tn(logit_grad, around.astype(BF16))
    values = middle[...]
    inverse = lax.rsqrt(jnp.mean(values * values, axis=-1, keepdims=True) + EPSILON)
    gain_grad = jnp.sum(grad * values * inverse, axis=0, keepdims=True)
    row = lax.broadcasted_iota(jnp.int32, (8, width), 0)
    rows8[...] = jnp.where(row == 1, gain_grad, router_grad)
    scaled = grad * around[1:2]
    result = (
        gysrc[:, :block].reshape(local, width).astype(F32)
        + inverse * scaled
        - values * inverse * inverse * inverse * jnp.mean(scaled * values, axis=-1, keepdims=True)
    )
    middle_grad[...] = result
    upstream = result.astype(BF16)
    for member in range(plan.quad):
        part = nt(upstream, w_mix[member * cols : (member + 1) * cols])
        dmixed[member] = part.astype(BF16).reshape(2, block, cols)
    return upstream


def front_kernel(plan, length_ref, tok, wq, win, gyw, cosine, sine, xs, w_seq, normed, qk_out, v_out, lse_out, mixed, gyall, w_in, gysrc, *rest):
    owned, rest = (rest[:4], rest[4:]) if plan.tiled else ((), rest)
    front_body(plan, length_ref, tok, wq, win, gyw, cosine, sine, xs, w_seq, normed, qk_out, v_out, lse_out, mixed, gyall, w_in, gysrc, owned, *rest)


def front_body(plan, length_ref, tok, wq, win, gyw, cosine, sine, xs, w_seq, normed, qk_out, v_out, lse_out, mixed, gyall, w_in, gysrc, owned, wall, wqx, win_all, qkv, made, w_tail, x_send, x_recv, s_send, s_recv, q_send, q_recv, f_send, f_recv, z_send, z_recv, own_sem, tail_sem, m_send, m_recv, *gather_sem):
    dp, ctx = place()
    half, member = lax.div(ctx, plan.quad), lax.rem(ctx, plan.quad)
    far = (1 - half) * plan.quad + member
    flat, flat_far = dp * plan.ctx + ctx, dp * plan.ctx + far
    mine = dp * plan.quad + member
    grid = Grid(plan)
    spot = grid.here()
    here = (dp, ctx)
    across = (dp, far)
    targets = half_members(plan, mine)
    devices = [
        (lax.div(target, plan.quad), half * plan.quad + lax.rem(target, plan.quad))
        for target in targets
    ]
    members = quad_members(plan, half, member)
    highs, ys = grid.sizes["high"], grid.sizes["y"]
    meet(devices + [across])
    pending = []

    def send(*args):
        copy = remote(*args)
        copy.start()
        pending.append(copy)

    swap_x = remote(tok.at[1 - half], xs.at[ctx], s_send.at[0], s_recv.at[0], across)
    swap_w = remote(wq, wqx, s_send.at[1], s_recv.at[1], across)
    swap_gy = remote(gyw.at[1 - half], gysrc.at[1], s_send.at[2], s_recv.at[2], across)
    swap_x.start()
    swap_w.start()

    def member_of(high, low):
        return half * plan.quad + lax.rem(spot["high"] + high, highs) * 2 + lax.rem(spot["low"] + low, 2)

    def token_block(side, high):
        at = half if side == 0 else 1 - half
        return at * plan.quad + lax.rem(spot["high"] + high, highs) * 2 + spot["low"]

    def token_sends(side, source):
        block = token_block(side, 0)
        for step in range(1, highs):
            index = side * (highs - 1) + step - 1
            send(source, xs.at[block], x_send.at[0, index], x_recv.at[0, side, highs - step - 1], (dp, member_of(step, 0)))
        send(source, xs.at[block], x_send.at[1, side * highs], x_recv.at[1, side, 0], (dp, member_of(0, 1)))

    def token_forward(side):
        for high in range(1, highs):
            block = token_block(side, high)
            remote(xs.at[block], xs.at[block], x_send.at[0, 0], x_recv.at[0, side, high - 1], here).wait_recv()
            send(xs.at[block], xs.at[block], x_send.at[1, side * highs + high], x_recv.at[1, side, high], (dp, member_of(0, 1)))

    def slice_sends(side, source, block):
        for i, (peer, to) in enumerate(members):
            send(source.at[to], wall.at[block], q_send.at[0, side, i], q_recv.at[block], (dp, peer))

    core_device = grid.device(grid.moved(spot, "core", 1))
    counter = [0, 0]

    def slice_on(block, source, along_y):
        if along_y:
            for step in range(1, ys):
                send(source, wall.at[block], q_send.at[1, 0, counter[0]], q_recv.at[block], grid.device(grid.moved(spot, "y", step)))
                counter[0] += 1
        send(source, wall.at[block], q_send.at[1, 1, counter[1]], q_recv.at[block], core_device)
        counter[1] += 1

    def slice_wait(block):
        remote(wq.at[0], wall.at[block], q_send.at[0, 0, 0], q_recv.at[block], here).wait_recv()

    token_sends(0, tok.at[half])
    slice_sends(0, wq, flat)
    slice_on(flat, wq.at[member], True)
    gysrc[0] = gyw[pl.ds(half, 1)][0]
    xs[pl.ds(ctx, 1)] = tok[pl.ds(half, 1)]
    wall[pl.ds(flat, 1)] = wq[pl.ds(member, 1)]
    swap_x.wait()
    token_sends(1, xs.at[far])
    swap_w.wait()
    slice_sends(1, wqx, flat_far)
    slice_on(flat_far, wqx.at[member], True)
    swap_gy.start()
    token_forward(0)
    for i, (peer, _) in enumerate(members):
        block = dp * plan.ctx + peer
        slice_wait(block)
        slice_on(block, wall.at[block], True)
    token_forward(1)
    for _, to in members:
        block = dp * plan.ctx + (1 - half) * plan.quad + to
        slice_wait(block)
        slice_on(block, wall.at[block], True)
    wall[pl.ds(flat_far, 1)] = wqx[pl.ds(member, 1)]

    for i, (target, device) in enumerate(zip(targets, devices)):
        send(win.at[target], win_all.at[flat], f_send.at[i], f_recv.at[i], device)
    send(win.at[mine], win_all.at[flat], z_send.at[0], z_recv.at[0], across)
    win_all[pl.ds(flat, 1)] = win[pl.ds(mine, 1)]

    def columns_on(i):
        source = lax.rem(mine + plan.group - 1 - i, plan.group)
        block = lax.div(source, plan.quad) * plan.ctx + half * plan.quad + lax.rem(source, plan.quad)
        remote(win.at[0], win_all.at[block], f_send.at[0], f_recv.at[i], here).wait_recv()
        send(win_all.at[block], win_all.at[block], z_send.at[1 + i], z_recv.at[1 + i], across)

    for step in range(1, ys):
        other = lax.rem(spot["y"] + step, ys) * 2 + spot["core"]
        for place_ctx in range(plan.ctx):
            block = other * plan.ctx + place_ctx
            slice_wait(block)
            slice_on(block, wall.at[block], False)
    swap_gy.wait()
    gather = Gather(grid, spot, gysrc, gyall, *gather_sem)
    own = pltpu.make_async_copy(gysrc, gyall.at[grid.block(spot)], own_sem)
    own.start()
    gather.level(0)
    for y in range(ys):
        for place_ctx in range(plan.ctx):
            slice_wait((y * 2 + 1 - spot["core"]) * plan.ctx + place_ctx)
    for side in range(2):
        for high in range(highs):
            block = half if side == 0 else 1 - half
            block = block * plan.quad + lax.rem(spot["high"] + high, highs) * 2 + 1 - spot["low"]
            remote(xs.at[block], xs.at[block], x_send.at[0, 0], x_recv.at[1, side, high], here).wait_recv()

    length = length_ref[0]
    rows, block = QUERY_ROWS, plan.block
    slots = plan.slots
    w_seq[...] = natural_rows(plan, wall[...])
    tail = w_seq[:, plan.wide - 128 :].astype(F32)
    gain = jnp.transpose(tail, (1, 0))[plan.qkv_cols - plan.wide + 128 :][:1]

    @pl.loop(0, slots // rows)
    def _(i):
        at = pl.ds(pl.multiple_of(i * rows, rows), rows)
        values = xs[pl.ds(i * (rows // block), rows // block)].reshape(rows, plan.width)
        values = values.astype(F32)
        inverse = lax.rsqrt(jnp.mean(values * values, axis=-1, keepdims=True) + EPSILON)
        normed[at] = (values * inverse * gain).astype(BF16)
        qkv[at] = nn(normed[at], w_seq[...])
    heads = plan.heads
    qk_width = 2 * HEAD_DIM
    third = (plan.group - 1) // 3
    for i in range(third):
        columns_on(i)
    for head in range(heads):
        cols = slice(head * qk_width, (head + 1) * qk_width)
        qk = qkv[:, cols]
        qk_out[:, cols] = (qk * cosine[...] + swapped_halves(qk) * sine[...]).astype(BF16)
    v_cols = slice(heads * qk_width, heads * 3 * HEAD_DIM)
    v_out[...] = qkv[:, v_cols].astype(BF16)
    gather.level(1)
    for i in range(third, 2 * third):
        columns_on(i)

    def mixed_copy(index):
        side, to = divmod(index, plan.quad)
        turn = lax.rem(half + side, 2)
        return remote(
            made.at[index],
            mixed.at[member, turn],
            m_send.at[index],
            m_recv.at[member, turn],
            (dp, half * plan.quad + to),
        )

    spans = list(range(0, slots, rows))
    for number, start in enumerate(spans):
        at = slice(start, start + rows)
        end = start + rows
        for head in range(heads):
            base = head * qk_width
            q = qk_out[at, base : base + HEAD_DIM] * BF16(0.125)
            k = qk_out[:end, base + HEAD_DIM : base + qk_width]
            v = v_out[:end, head * HEAD_DIM : (head + 1) * HEAD_DIM]
            scores = masked_scores(q, k, start, length)
            top = jnp.max(scores, axis=-1, keepdims=True)
            raised = jnp.exp(scores - top)
            total = jnp.sum(raised, axis=-1, keepdims=True)
            lse_out[head, at] = top + jnp.log(total)
            probs = (raised * (1.0 / total)).astype(BF16)
            part = nn(probs, v).astype(BF16)
            for i in range(rows // block):
                made[start // block + i, :, head * HEAD_DIM : (head + 1) * HEAD_DIM] = part[
                    i * block : (i + 1) * block
                ]
        for i in range(rows // block):
            index = start // block + i
            pl.when(member != index % plan.quad)(lambda index=index: mixed_copy(index).start())

            @pl.when(member == index % plan.quad)
            def _(index=index):
                turn = lax.rem(half + index // plan.quad, 2)
                mixed[pl.ds(member, 1), pl.ds(turn, 1)] = made[index][None, None]

        if number == len(spans) // 2:
            for i in range(2 * third, plan.group - 1):
                columns_on(i)
            gather.level(2)
    gather.level(3)
    for index in range(plan.ctx):
        pl.when(member != index % plan.quad)(lambda index=index: mixed_copy(index).wait_send())
    for source in range(plan.quad):

        @pl.when(member != source)
        def _(source=source):
            for turn in range(2):
                remote(
                    made.at[0], mixed.at[source, turn], m_send.at[0], m_recv.at[source, turn], here
                ).wait_recv()

    gather.finish()
    own.wait()
    if owned:
        load = pltpu.make_async_copy(gyall.at[:, :, plan.block :], w_tail, tail_sem)
        load.start()
        load.wait()
        owner_forward(plan, ctx, far, half, xs, w_seq, mixed, gysrc, w_tail, *owned)
    for copy in pending:
        copy.wait_send()
    for i in range(plan.group):
        remote(win.at[0], win_all.at[0], z_send.at[0], z_recv.at[i], here).wait_recv()
    pad, hidden = plan.pad_rows, plan.hidden_pad
    if plan.tiled:
        count = plan.quad * plan.rows

        @pl.loop(0, plan.devices // plan.quad)
        def _(i):
            at = pl.ds(pl.multiple_of(i * count, 16), count)
            value = win_all[pl.ds(i * plan.quad, plan.quad)].astype(F32)
            for gate in range(2):
                part = value[:, gate * pad : (gate + 1) * pad].reshape(count, hidden)
                w_in[at, gate * hidden : (gate + 1) * hidden] = part.astype(BF16)

    else:
        w_in[:, :hidden] = natural_rows(plan, win_all[:, :pad])
        w_in[:, hidden:] = natural_rows(plan, win_all[:, pad:])


def front(plan, length, tok, wq, win, gyw, cosine, sine, collective_id):
    slots, heads, block, width = plan.slots, plan.heads, plan.block, plan.width
    highs, ys = plan.quad // 2, plan.dp // 2
    owned = (
        jax.ShapeDtypeStruct((plan.local + MIX_ROWS, width), BF16),
        jax.ShapeDtypeStruct((plan.local, width), F32),
        jax.ShapeDtypeStruct((8, plan.local), F32),
        jax.ShapeDtypeStruct((width, width), BF16),
    )
    on = max(2 * plan.quad * max(ys - 1, 1), 2 * plan.quad + (ys - 1) * plan.ctx, plan.quad)
    return pl.pallas_call(
        functools.partial(front_kernel, plan),
        out_shape=(
            jax.ShapeDtypeStruct((plan.ctx, block, width), BF16),
            jax.ShapeDtypeStruct((width, plan.wide), BF16),
            jax.ShapeDtypeStruct((slots, width), BF16),
            jax.ShapeDtypeStruct((slots, 2 * plan.head_cols), BF16),
            jax.ShapeDtypeStruct((slots, plan.head_cols), BF16),
            jax.ShapeDtypeStruct((heads, slots, 1), F32),
            jax.ShapeDtypeStruct((plan.quad, 2, block, plan.head_cols), BF16),
            jax.ShapeDtypeStruct((plan.group, 2) + gyw.shape[1:], BF16),
            jax.ShapeDtypeStruct((width, 2 * plan.hidden_pad), BF16),
            jax.ShapeDtypeStruct(gyw.shape, BF16),
        )
        + (owned if plan.tiled else ()),
        in_specs=[pl.BlockSpec(memory_space=pltpu.SMEM)] + [VMEM] * 6,
        out_specs=(VMEM,) * 7 + (HBM,) + (VMEM,) * (6 if plan.tiled else 2),
        scratch_shapes=[
            pltpu.VMEM((plan.devices,) + wq.shape[1:], BF16),
            pltpu.VMEM(wq.shape, BF16),
            pltpu.VMEM((plan.devices,) + win.shape[1:], BF16),
            pltpu.VMEM((slots, plan.wide), F32),
            pltpu.VMEM((plan.ctx, block, plan.head_cols), BF16),
            pltpu.VMEM((plan.group, 2, gyw.shape[1] - block, width), BF16),
            DMA((2, 2 * highs)),
            DMA((2, 2, highs)),
            DMA((3,)),
            DMA((3,)),
            DMA((2, 2, on)),
            DMA((plan.devices,)),
            DMA((plan.group - 1,)),
            DMA((plan.group - 1,)),
            DMA((plan.group,)),
            DMA((plan.group,)),
            DMA,
            DMA,
            DMA((plan.ctx,)),
            DMA((plan.quad, 2)),
        ]
        + gather_sems(plan),
        compiler_params=params(collective_id),
        cost_estimate=busy(90),
        name="front",
    )(length, tok, wq, win, gyw, cosine, sine)


OUT_ORDERS = (("low", "y", "high"), ("y", "low", "high"))


class OutSum:
    def __init__(self, grid, at, src, work, core_buf, bufs, load_sem, core_send, core_recv, send, recv):
        self.grid, self.at, self.src = grid, at, src
        self.work, self.core_buf, self.bufs = work, core_buf, bufs
        self.load_sem, self.core_send, self.core_recv = load_sem, core_send, core_recv
        self.send, self.recv = send, recv
        self.loaded = set()
        rows = work.shape[1] // 2
        self.rows = [slice(0, rows), slice(rows, 2 * rows)]
        self.index = [
            {o: i for i, o in enumerate(o for o in STEP_ORDER if any(o))} for _ in OUT_ORDERS
        ]

    def pair(self, offset):
        where = dict(self.at)
        for axis, step in named(offset).items():
            if step:
                where = self.grid.moved(where, axis, step)
        slot = self.grid.slot(named(offset))
        partner = self.grid.device(self.grid.moved(self.at, "core", 1))
        away = remote(
            self.src.at[self.grid.block(self.grid.moved(where, "core", 1))],
            self.core_buf.at[slot],
            self.core_send.at[slot],
            self.core_recv.at[slot],
            partner,
        )
        load = pltpu.make_async_copy(
            self.src.at[self.grid.block(where)], self.work.at[slot], self.load_sem.at[slot]
        )
        return away, load

    def start(self):
        for offset in STEP_ORDER[::-1]:
            for copy in self.pair(offset):
                copy.start()

    def onward(self, part, offset, axis):
        index, rows = self.index[part][offset], self.rows[part]
        return remote(
            self.work.at[self.grid.slot(named(offset)), rows],
            self.bufs.at[index, rows],
            self.send.at[part, index],
            self.recv.at[part, index],
            self.grid.device(self.grid.moved(self.at, axis, 1)),
        )

    def phase(self, number):
        for offset in STEP_ORDER:
            for part, order in enumerate(OUT_ORDERS):
                phase, feeds = feeds_of(order, offset)
                if phase != number:
                    continue
                if offset not in self.loaded:
                    self.loaded.add(offset)
                    for copy in self.pair(offset):
                        copy.wait()
                for feed, axis in zip(feeds, order):
                    self.onward(part, feed, axis).wait_recv()
                slot, rows = self.grid.slot(named(offset)), self.rows[part]

                @pl.loop(0, (rows.stop - rows.start) // 16)
                def _(i, slot=slot, part=part, feeds=feeds, start=rows.start):
                    span = pl.ds(pl.multiple_of(start + i * 16, 16), 16)
                    value = self.work[slot, span].astype(F32)
                    value = value + self.core_buf[slot, span].astype(F32)
                    for feed in feeds:
                        value = value + self.bufs[self.index[part][feed], span].astype(F32)
                    self.work[slot, span] = value.astype(BF16)

                if number < 3:
                    self.onward(part, offset, order[number]).start()

    def finish(self):
        for offset in STEP_ORDER:
            for part, order in enumerate(OUT_ORDERS):
                phase, _ = feeds_of(order, offset)
                if phase < 3:
                    self.onward(part, offset, order[phase]).wait_send()


class Fold:
    def __init__(self, plan, src, dst, core_buf, y_buf, added, sems):
        self.plan, self.src, self.dst = plan, src, dst
        self.core_buf, self.y_buf, self.added = core_buf, y_buf, added
        self.core_send, self.core_recv, self.y_send, self.y_recv, self.send, self.recv = sems
        self.dp, self.ctx = place()
        self.core, self.y = lax.rem(self.dp, 2), lax.div(self.dp, 2)
        self.ys = plan.dp // 2

    def core_copies(self):
        partner = (self.dp + 1 - 2 * self.core, self.ctx)
        return [
            remote(
                self.src.at[y * 2 + 1 - self.core],
                self.core_buf.at[y],
                self.core_send.at[y],
                self.core_recv.at[y],
                partner,
            )
            for y in range(self.ys)
        ]

    def y_copies(self):
        copies = []
        for step in range(1, self.ys):
            to = lax.rem(self.y + step, self.ys)
            copies.append(
                remote(
                    self.core_buf.at[to],
                    self.y_buf.at[step - 1],
                    self.y_send.at[step - 1],
                    self.y_recv.at[step - 1],
                    (to * 2 + self.core, self.ctx),
                )
            )
        return copies

    def owner_copies(self):
        copies = []
        for step in range(1, self.plan.ctx):
            to = lax.rem(self.ctx + step, self.plan.ctx)
            copies.append(
                remote(
                    self.added.at[to],
                    self.dst.at[self.ctx],
                    self.send.at[step - 1],
                    self.recv.at[step - 1],
                    (self.dp, to),
                )
            )
        return copies

    def start(self):
        for copy in self.core_copies():
            copy.start()

    def along_y(self):
        for copy in self.core_copies():
            copy.wait()

        @pl.loop(0, self.plan.ctx)
        def _(i):
            for y in range(self.ys):
                mine = self.src[y * 2 + self.core, i].astype(F32)
                self.core_buf[y, i] = (mine + self.core_buf[y, i].astype(F32)).astype(BF16)

        for copy in self.y_copies():
            copy.start()

    def to_owners(self):
        for copy in self.y_copies():
            copy.wait()

        @pl.loop(0, self.plan.ctx)
        def _(i):
            total = self.core_buf[self.y, i].astype(F32)
            for step in range(1, self.ys):
                total = total + self.y_buf[step - 1, i].astype(F32)
            self.added[i] = total.astype(BF16)

        for copy in self.owner_copies():
            copy.start()
        self.dst[pl.ds(self.ctx, 1)] = self.added[pl.ds(self.ctx, 1)]

    def finish(self):
        for copy in self.owner_copies():
            copy.wait()


def padded_rows(plan, value, count):
    if plan.pad_rows != plan.rows:
        row = lax.broadcasted_iota(jnp.int32, (count * plan.pad_rows, count * plan.rows), 0)
        col = lax.broadcasted_iota(jnp.int32, (count * plan.pad_rows, count * plan.rows), 1)
        inside = lax.rem(row, plan.pad_rows)
        wanted = lax.div(row, plan.pad_rows) * plan.rows + inside
        hit = (col == wanted) & (inside < plan.rows)
        value = nn(hit.astype(BF16), value.astype(BF16))
    return value.reshape(count, plan.pad_rows, value.shape[-1])


def fold_scratch(plan, rows, width):
    shape = (plan.ctx, rows, width)
    ys = plan.dp // 2
    return [
        pltpu.VMEM((ys,) + shape, BF16),
        pltpu.VMEM((max(ys - 1, 1),) + shape, BF16),
        pltpu.VMEM(shape, BF16),
        DMA((ys,)),
        DMA((ys,)),
        DMA((max(ys - 1, 1),)),
        DMA((max(ys - 1, 1),)),
        DMA((plan.ctx - 1,)),
        DMA((plan.ctx - 1,)),
    ]


def back_kernel(plan, summed, length_ref, x, w, cosine, sine, normed, qk_in, v_in, lse, dw_in, dw_out, out_part, middle, *rest):
    given = 6 if plan.tiled else 4
    back_body(plan, summed, length_ref, x, w, cosine, sine, normed, qk_in, v_in, lse, dw_in, dw_out, out_part, middle, rest[:given], *rest[given:])


def back_body(plan, summed, length_ref, x, w, cosine, sine, normed, qk_in, v_in, lse, dw_in, dw_out, out_part, middle, given, rwq, rwo, rwin, far_out, act_out, grad_out, dqkv, dk_acc, dv_acc, upstream_all, dnp, rdn, dwq, far_in, dealt, out_away, grad_away, act_away, d_send, d_recv, n_send, n_recv, w_send, w_recv, e_send, e_recv, s_send, s_recv, *refs):
    dp, ctx = place()
    core, y = lax.rem(dp, 2), lax.div(dp, 2)
    half, member = lax.div(ctx, plan.quad), lax.rem(ctx, plan.quad)
    far = (1 - half) * plan.quad + member
    mine = dp * plan.quad + member
    across = (dp, far)
    members = quad_members(plan, half, member)
    targets = half_members(plan, mine)
    devices = [
        (lax.div(target, plan.quad), half * plan.quad + lax.rem(target, plan.quad))
        for target in targets
    ]
    meet(
        devices
        + [across]
        + [
            (dp, (1 - half) * plan.quad + lax.rem(member + step, plan.quad))
            for step in range(1, plan.quad)
        ]
    )
    fold_refs, out_refs = refs[:18], refs[18:]
    out_sum = None
    if not summed:
        grid = Grid(plan)
        out_sum = OutSum(grid, grid.here(), out_part, *out_refs[:8])
        out_sum.start()
    if plan.tiled:
        n2g_sum, gates, n2x, gysrc, w_mix, mixed = given
        dmixed, dwo, rows8, middle_grad = out_refs[8:]
        attn_grad = owner_back(plan, n2g_sum, gates, n2x, gysrc, w_mix, mixed, middle, w, *out_refs[8:])
    else:
        dmixed, dwo, small, middle_grad = given
    arriving = []
    for i, (peer, to) in enumerate(members):
        for j, at in enumerate((ctx, far)):
            copy = remote(
                dmixed.at[to, j],
                upstream_all.at[at],
                d_send.at[2 * i + j],
                d_recv.at[2 * i + j],
                (dp, peer),
            )
            copy.start()
            arriving.append(copy)
    count = len(fold_refs) // 2
    mix_fold = Fold(plan, dwo, rwo, *fold_refs[:3], fold_refs[3:count])
    qkv_fold = Fold(plan, dwq, rwq, *fold_refs[count : count + 3], fold_refs[count + 3 :])
    if plan.tiled:
        for i in range(plan.quad):
            part = tn(mixed[i].reshape(plan.local, plan.head_cols), attn_grad)
            dwo[i] = padded_rows(plan, part, plan.ctx).astype(BF16)
    mix_fold.start()
    swaps = [
        remote(dw_in.at[2 * i + 1 - half], far_in.at[i], w_send.at[i], w_recv.at[i], across)
        for i in range(plan.dp)
    ]
    hidden, pad = plan.hidden_pad, plan.pad_rows

    def deal_copy(target):
        tdp, tmember = divmod(target, plan.quad)
        return remote(
            dealt.at[target],
            rwin.at[mine],
            e_send.at[target],
            e_recv.at[mine],
            (tdp, half * plan.quad + tmember),
        )

    def deal(i):
        swaps[i].wait()
        value = dw_in[pl.ds(2 * i + half, 1)][0].astype(F32) + far_in[i].astype(F32)
        value = padded_rows(plan, value, plan.quad)
        value = jnp.concatenate([value[:, :, :hidden], value[:, :, hidden:]], axis=1)
        dealt[i * plan.quad : (i + 1) * plan.quad] = value.astype(BF16)
        for target in range(i * plan.quad, (i + 1) * plan.quad):
            pl.when(mine != target)(lambda target=target: deal_copy(target).start())

            @pl.when(mine == target)
            def _(target=target):
                rwin[target] = dealt[target]

    for copy in swaps:
        copy.start()
    out_away[...] = dw_out[:, pl.ds(1 - half, 1)][:, 0].astype(BF16)
    swap_out = remote(out_away, far_out, s_send.at[2], s_recv.at[2], across)
    upstream_all[pl.ds(ctx, 1)] = dmixed[pl.ds(member, 1), 0]
    upstream_all[pl.ds(far, 1)] = dmixed[pl.ds(member, 1), 1]
    length = length_ref[0]
    rows, slots, heads, block = QUERY_ROWS, plan.slots, plan.heads, plan.block
    qk_width = 2 * HEAD_DIM
    dqkv[...] = jnp.zeros_like(dqkv)
    for copy in arriving:
        copy.wait()

    def token_copy(index):
        side, to = divmod(index, plan.quad)
        turn = lax.rem(half + side, 2)
        return remote(
            dnp.at[index],
            rdn.at[member, turn],
            n_send.at[index],
            n_recv.at[member, turn],
            (dp, half * plan.quad + to),
        )

    gains = jnp.zeros((1, plan.width), F32)
    spans = list(range(slots - rows, -1, -rows))
    for number, start in enumerate(spans):
        at = slice(start, start + rows)
        end = start + rows
        for head in range(heads):
            base = head * qk_width
            v_cols = slice(head * HEAD_DIM, (head + 1) * HEAD_DIM)
            q = qk_in[at, base : base + HEAD_DIM] * BF16(0.125)
            k = qk_in[:end, base + HEAD_DIM : base + qk_width]
            v = v_in[:end, v_cols]
            upstream = jnp.concatenate(
                [upstream_all[start // block + i, :, v_cols] for i in range(rows // block)], axis=0
            )
            probs = jnp.exp(masked_scores(q, k, start, length) - lse[head, at])
            dv = tn(probs.astype(BF16), upstream)
            prob_grad = nt(upstream, v)
            inner = jnp.sum(probs * prob_grad, axis=-1, keepdims=True)
            score_grad = (probs * (prob_grad - inner)).astype(BF16)
            dq = nn(score_grad, k) * 0.125
            dk = tn(score_grad, q)
            if end == slots:
                dk_acc[head] = dk
                dv_acc[head] = dv
            else:
                dk_acc[head, :end] += dk
                dv_acc[head, :end] += dv
            dqk = jnp.concatenate([dq, dk_acc[head, at]], axis=-1)
            dqkv[at, base : base + qk_width] = (
                dqk * cosine[at] - swapped_halves(dqk) * sine[at]
            ).astype(BF16)
            v_base = heads * qk_width + head * HEAD_DIM
            dqkv[at, v_base : v_base + HEAD_DIM] = dv_acc[head, at].astype(BF16)
        part = nt(dqkv[at], w[...])
        for i in range(rows // block):
            index = start // block + i
            dnp[index] = part[i * block : (i + 1) * block].astype(BF16)
            pl.when(member != index % plan.quad)(lambda index=index: token_copy(index).start())

            @pl.when(member == index % plan.quad)
            def _(index=index):
                turn = lax.rem(half + index // plan.quad, 2)
                rdn[pl.ds(member, 1), pl.ds(turn, 1)] = dnp[index][None, None]

        values = x[at].astype(F32)
        inverse = lax.rsqrt(jnp.mean(values * values, axis=-1, keepdims=True) + EPSILON)
        gains = gains + jnp.sum(part * values * inverse, axis=0, keepdims=True)
        if number == 0:
            mix_fold.along_y()
            if out_sum:
                out_sum.phase(0)
        if number == len(spans) - 2:
            mix_fold.to_owners()
            if out_sum:
                out_sum.phase(1)
    swap_out.start()
    deal(0)
    first = plan.qkv_cols - (plan.wide - 128)
    if plan.tiled:
        row = lax.broadcasted_iota(jnp.int32, (8, plan.width), 0)
        ends = [jnp.zeros((n, plan.width), F32) for n in (first, 120 - first)]
        extra = jnp.concatenate([ends[0], jnp.where(row == 0, gains, rows8[...]), ends[1]], axis=0)
        extra = jnp.transpose(extra, (1, 0))
    else:
        column = jnp.transpose(jnp.broadcast_to(gains, (128, plan.width)), (1, 0))
        lane = lax.broadcasted_iota(jnp.int32, column.shape, 1)
        extra = jnp.where(lane == first, column, small[...])
    last = plan.wide // 128 - 1

    @pl.loop(0, last + 1)
    def _(i):
        cols = pl.ds(pl.multiple_of(i * 128, 128), 128)
        value = tn(normed[...], dqkv[:, cols])
        value = jnp.where(i == last, value + extra, value)
        value = padded_rows(plan, value, plan.devices).astype(BF16)
        dwq[:, :, :, cols] = value.reshape(plan.dp, plan.ctx, plan.pad_rows, 128)

    qkv_fold.start()
    local, width = plan.local, plan.width
    if out_sum:
        out_sum.phase(2)
    for source in range(plan.quad):

        @pl.when(member != source)
        def _(source=source):
            for turn in range(2):
                remote(
                    dnp.at[0], rdn.at[source, turn], n_send.at[0], n_recv.at[source, turn], (dp, ctx)
                ).wait_recv()

    gain_row = around_gains(plan, w)[:1]
    piece = 32

    for j, own in enumerate((ctx, far)):

        @pl.loop(0, block // piece)
        def _(i, j=j, own=own):
            rows_in = pl.ds(pl.multiple_of(i * piece, piece), piece)
            total = rdn[0, j, rows_in].astype(F32)
            for source in range(1, plan.quad):
                total = total + rdn[source, j, rows_in].astype(F32)
            values = x[pl.ds(pl.multiple_of(own * block + i * piece, piece), piece)].astype(F32)
            inverse = lax.rsqrt(jnp.mean(values * values, axis=-1, keepdims=True) + EPSILON)
            scaled = total * gain_row
            result = (
                middle_grad[pl.ds(pl.multiple_of(j * block + i * piece, piece), piece)]
                + inverse * scaled
                - values
                * inverse
                * inverse
                * inverse
                * jnp.mean(scaled * values, axis=-1, keepdims=True)
            )
            if j == 0:
                grad_out[pl.ds(half, 1), rows_in] = result.astype(BF16)[None]
            else:
                grad_away[rows_in] = result.astype(BF16)

    swap_grad = remote(grad_away, grad_out.at[half], s_send.at[1], s_recv.at[1], across)
    swap_grad.start()
    qkv_fold.along_y()
    if out_sum:
        out_sum.phase(3)
    branches = out_sum.work.at[0] if out_sum else out_part

    for j in range(2):

        @pl.loop(0, block // piece)
        def _(i, j=j):
            rows_in = pl.ds(pl.multiple_of(i * piece, piece), piece)
            rows_all = pl.ds(pl.multiple_of(j * block + i * piece, piece), piece)
            value = (middle[rows_all] + branches[rows_all].astype(F32)).astype(BF16)
            if j == 0:
                act_out[pl.ds(half, 1), rows_in] = value[None]
            else:
                act_away[rows_in] = value

    swap_act = remote(act_away, act_out.at[half], s_send.at[0], s_recv.at[0], across)
    swap_act.start()
    for i in range(1, plan.dp):
        deal(i)
        if i == 1:
            qkv_fold.to_owners()
    mix_fold.finish()
    qkv_fold.finish()
    swap_act.wait()
    swap_grad.wait()
    swap_out.wait()
    for target in range(plan.group):

        @pl.when(mine != target)
        def _(target=target):
            deal_copy(target).wait_send()
            remote(
                dealt.at[0], rwin.at[target], e_send.at[0], e_recv.at[target], (dp, ctx)
            ).wait_recv()

    for index in range(plan.ctx):
        pl.when(member != index % plan.quad)(lambda index=index: token_copy(index).wait_send())
    if out_sum:
        out_sum.finish()


def back(plan, length, x, w, cosine, sine, normed, qk, v, lse, dw_in, dw_out, out_part, middle, given, collective_id):
    slots, block, width = plan.slots, plan.block, plan.width
    count = 2 * (plan.quad - 1)
    dealt = (plan.group, 2 * plan.pad_rows, plan.hidden_pad)
    summed = out_part.ndim == 2
    rows = (plan.local, width)
    out_scratch = [
        pltpu.VMEM((8,) + rows, BF16),
        pltpu.VMEM((8,) + rows, BF16),
        pltpu.VMEM((7,) + rows, BF16),
        DMA((8,)),
        DMA((8,)),
        DMA((8,)),
        DMA((2, 7)),
        DMA((2, 7)),
        pltpu.VMEM((plan.quad, 2, block, plan.head_cols), BF16),
        pltpu.VMEM((plan.dp, plan.ctx, plan.rows, width), BF16),
        pltpu.VMEM((8, width), F32),
        pltpu.VMEM((plan.local, width), F32),
    ]
    return pl.pallas_call(
        functools.partial(back_kernel, plan, summed),
        out_shape=(
            jax.ShapeDtypeStruct((plan.ctx, plan.pad_rows, plan.wide), BF16),
            jax.ShapeDtypeStruct((plan.ctx, plan.rows, width), BF16),
            jax.ShapeDtypeStruct(dealt, BF16),
            jax.ShapeDtypeStruct((plan.branches, plan.own_hidden, width), BF16),
            jax.ShapeDtypeStruct((2, block, width), BF16),
            jax.ShapeDtypeStruct((2, block, width), BF16),
        ),
        in_specs=[pl.BlockSpec(memory_space=pltpu.SMEM)]
        + [VMEM] * 10
        + [VMEM if summed else HBM]
        + [VMEM] * (1 + len(given)),
        out_specs=(VMEM,) * 6,
        scratch_shapes=[
            pltpu.VMEM((slots, plan.wide), BF16),
            pltpu.VMEM((plan.heads, slots, HEAD_DIM), F32),
            pltpu.VMEM((plan.heads, slots, HEAD_DIM), F32),
            pltpu.VMEM((plan.ctx, block, plan.head_cols), BF16),
            pltpu.VMEM((plan.ctx, block, width), BF16),
            pltpu.VMEM((plan.quad, 2, block, width), BF16),
            pltpu.VMEM((plan.dp, plan.ctx, plan.pad_rows, plan.wide), BF16),
            pltpu.VMEM((plan.dp,) + dw_in.shape[1:], BF16),
            pltpu.VMEM(dealt, BF16),
            pltpu.VMEM((plan.branches, plan.own_hidden, width), BF16),
            pltpu.VMEM((block, width), BF16),
            pltpu.VMEM((block, width), BF16),
            DMA((count,)),
            DMA((count,)),
            DMA((plan.ctx,)),
            DMA((plan.quad, 2)),
            DMA((plan.dp,)),
            DMA((plan.dp,)),
            DMA((plan.group,)),
            DMA((plan.group,)),
            DMA((3,)),
            DMA((3,)),
        ]
        + fold_scratch(plan, plan.rows, width)
        + fold_scratch(plan, plan.pad_rows, plan.wide)
        + ([] if summed else out_scratch),
        compiler_params=params(collective_id),
        cost_estimate=busy(90),
        name="back",
    )(length, x, w, cosine, sine, normed, qk, v, lse, dw_in, dw_out, out_part, middle, *given)


def ffn_kernel(plan, members, n2x, gy, w_in, w_out, pick, out, n2g, dw_in, dw_out):
    hidden, local = plan.hidden_pad, plan.local

    @pl.when(pl.program_id(0) == 0)
    def start():
        dw_in[...] = jnp.zeros_like(dw_in)
        dw_out[...] = jnp.zeros_like(dw_out)

    tokens = members * local
    width = plan.width
    normed = n2x[:, :local].reshape(tokens, width)
    upstream = gy[:, :, : plan.block].reshape(tokens, width)
    mixing = jnp.concatenate(
        [tn(n2x[i, local:, :local], pick[...]) for i in range(members)], axis=0
    )
    pre = nn(normed, w_in[...])
    gate, up = pre[:, :hidden], pre[:, hidden:]
    sigmoid = jax.nn.sigmoid(gate)
    silu = gate * sigmoid
    act = (silu * up).astype(BF16).astype(F32)
    act_mixed = (act * mixing).astype(BF16)
    out[...] = nn(act_mixed, w_out[...]).astype(BF16).reshape(members, local, width)
    act_grad = nt(upstream, w_out[...])
    choice = nt(pick[...], (act * act_grad).astype(BF16)).astype(BF16)
    act_grad = act_grad * mixing
    gate_grad = act_grad * up * sigmoid * (1.0 + gate * (1.0 - sigmoid))
    pre_grad = jnp.concatenate([gate_grad, act_grad * silu], axis=-1).astype(BF16)
    n2g[:, :local] = nt(pre_grad, w_in[...]).astype(BF16).reshape(members, local, width)
    pad = jnp.zeros((MIX_ROWS, width - local), BF16)
    for i in range(members):
        n2g[i, local:] = jnp.concatenate(
            [choice[:, i * local : (i + 1) * local], pad], axis=-1
        )
    dw_in[...] += tn(normed, pre_grad)
    dw_out[...] += tn(act_mixed, upstream)


def ffn(plan, n2x, gy, w_in, w_out, pick):
    members = 2
    local, width, hidden = plan.local, plan.width, plan.hidden_pad
    whole = lambda i: (0, 0)
    part = lambda i: (i, 0, 0)
    return pl.pallas_call(
        functools.partial(ffn_kernel, plan, members),
        grid=(plan.group // members,),
        out_shape=(
            jax.ShapeDtypeStruct((plan.group, local, width), BF16),
            jax.ShapeDtypeStruct((plan.group, local + MIX_ROWS, width), BF16),
            jax.ShapeDtypeStruct((width, 2 * hidden), F32),
            jax.ShapeDtypeStruct((hidden, width), F32),
        ),
        in_specs=[
            pl.BlockSpec((members, local + MIX_ROWS, width), part),
            pl.BlockSpec((members,) + gy.shape[1:], lambda i: (i, 0, 0, 0)),
            pl.BlockSpec((width, 2 * hidden), whole),
            pl.BlockSpec((hidden, width), whole),
            pl.BlockSpec((MIX_ROWS, hidden), whole),
        ],
        out_specs=(
            pl.BlockSpec((members, local, width), part),
            pl.BlockSpec((members, local + MIX_ROWS, width), part),
            pl.BlockSpec((width, 2 * hidden), whole),
            pl.BlockSpec((hidden, width), whole),
        ),
        compiler_params=params(),
        name="ffn",
    )(n2x, gy, w_in, w_out, pick)


STEP_ORDER = ((0, 0, 0), (0, 0, 1), (0, 1, 0), (1, 0, 1), (1, 1, 0), (1, 1, 1), (0, 1, 1), (1, 0, 0))
PART_ORDERS = (("high", "low", "y"), ("low", "y", "high"), ("y", "high", "low"))
PAUSES = {
    3: (('g0', 7), ('g0', 2), ('g0', 1), ('g1', 1), ('g2', 1)),
    4: (('g1', 2), ('g2', 7), ('g2', 2), ('g1', 7)),
    5: (('g0', 4), ('g0', 3), ('g1', 3)),
    7: (('g2', 3), ('g0', 6), ('g2', 6), ('s2', 1)),
    8: (('g1', 4), ('g2', 4)),
    9: (('g1', 6),),
    10: (('s1', 2),),
    11: (('g0', 5), ('g2', 5)),
    13: (('g1', 5), ('s0', 3), ('s2', 3)),
    16: (('s0', 4), ('s1', 4)),
    19: (('s0', 5), ('s1', 5), ('s2', 5)),
    20: (('s0', 2),),
    22: (('s1', 6), ('s2', 6)),
    23: (('s1', 3), ('s2', 4), ('s0', 6)),
    24: (('s0', 7), ('s2', 7), ('s1', 1), ('s2', 2), ('s1', 7), ('s0', 1), ('s2', 0), ('s0', 0), ('s1', 0)),
}


def part_rows(rows):
    cuts = [round_up(rows * i // 3, 16) for i in range(3)] + [rows]
    return [slice(a, b) for a, b in zip(cuts, cuts[1:])]


def named(offset):
    return dict(zip(("high", "low", "y"), offset))


def feeds_of(order, offset):
    at = named(offset)
    phase = min([i for i, axis in enumerate(order) if at[axis]], default=3)
    names = ("high", "low", "y")
    return phase, [tuple(1 if n == axis else at[n] for n in names) for axis in order[:phase]]


def fused_kernel(plan, n2x, gy, w_in, w_out, pick, total, dw_in, dw_out, out_all, n2all, gybuf, acc, away, work, core_buf, bufs, outbuf, gy_sem, out_sem, g_send, g_recv, gc_send, gc_recv, c_send, c_recv, r_send, r_recv):
    grid = Grid(plan)
    at = grid.here()
    local, width, hidden = plan.local, plan.width, plan.hidden_pad
    steps = len(STEP_ORDER)
    partner = grid.device(grid.moved(at, "core", 1))
    here = grid.device(at)
    parts = range(len(PART_ORDERS))
    in_rows, sum_rows = part_rows(local + MIX_ROWS), part_rows(local + MIX_ROWS)

    def absolute(offset):
        where = dict(at)
        for axis, step in named(offset).items():
            if step:
                where = grid.moved(where, axis, step)
        return where

    def slot_of(offset):
        return grid.slot(named(offset))

    def level_of(part, offset):
        reached = named(offset)
        return max([i + 1 for i, axis in enumerate(PART_ORDERS[part]) if reached[axis]], default=0)

    send_index = {}
    for part in parts:
        count = 0
        for offset in STEP_ORDER:
            for axis in PART_ORDERS[part][level_of(part, offset) :]:
                send_index[part, offset, axis] = count
                count += 1

    def pass_on(part, offset):
        level = level_of(part, offset)
        block = grid.block(absolute(offset))
        slot = slot_of(offset)
        span = in_rows[part]
        landing = n2all.at[block, span]
        if level:
            remote(landing, landing, g_send.at[part, 0], g_recv.at[part, slot], here).wait_recv()
        source = landing if level else n2x.at[span]
        for axis in PART_ORDERS[part][level:]:
            seen = grid.slot({**named(offset), axis: 1})
            remote(
                source,
                landing,
                g_send.at[part, send_index[part, offset, axis]],
                g_recv.at[part, seen],
                grid.device(grid.moved(at, axis, 1)),
            ).start()
        remote(source, landing, gc_send.at[part, slot], gc_recv.at[part, slot], partner).start()

    listed = [(kind[0], int(kind[1]), STEP_ORDER[place]) for row in PAUSES.values() for kind, place in row]
    buf_index, seen_slots, first_sums = {}, set(), set()
    for kind, part, offset in listed:
        if kind == "s":
            if offset not in seen_slots:
                seen_slots.add(offset)
                first_sums.add((part, offset))
            if any(offset):
                buf_index[part, offset] = sum(1 for other, _ in buf_index if other == part)

    def add_up(part, offset):
        phase, feeds = feeds_of(PART_ORDERS[part], offset)
        axis = PART_ORDERS[part][phase] if phase < 3 else None
        slot = slot_of(offset)
        span = sum_rows[part]
        if (part, offset) in first_sums:
            remote(away.at[0], core_buf.at[slot], c_send.at[0], c_recv.at[slot], here).wait_recv()
        for feed in feeds:
            index = buf_index[part, feed]
            ref = bufs.at[index, span]
            remote(ref, ref, r_send.at[part, 0], r_recv.at[part, index], here).wait_recv()

        @pl.loop(0, (span.stop - span.start) // 16)
        def _(i):
            rows = pl.ds(pl.multiple_of(span.start + i * 16, 16), 16)
            value = work[slot, rows].astype(F32) + core_buf[slot, rows].astype(F32)
            for feed in feeds:
                value = value + bufs[buf_index[part, feed], rows].astype(F32)
            if axis is None:
                total[rows] = value
            else:
                work[slot, rows] = value.astype(BF16)

        if axis is not None:
            index = buf_index[part, offset]
            remote(
                work.at[slot, span],
                bufs.at[index, span],
                r_send.at[part, index],
                r_recv.at[part, index],
                grid.device(grid.moved(at, axis, 1)),
            ).start()

    def pause(number):
        for kind, place in PAUSES.get(number, ()):
            act = pass_on if kind[0] == "g" else add_up
            act(int(kind[1]), STEP_ORDER[place])

    def pauses(step, turn):
        for i in range(steps):
            if 3 * i + turn in PAUSES:
                pl.when(step == i)(functools.partial(pause, 3 * i + turn))

    def bit(step, index):
        value = 0
        for i, offset in enumerate(STEP_ORDER):
            if offset[index]:
                value = value + jnp.where(step == i, 1, 0)
        return value

    def blocks_of(step):
        where = dict(at)
        offsets = {}
        for index, axis in enumerate(("high", "low", "y")):
            offsets[axis] = bit(step, index)
            where[axis] = lax.rem(at[axis] + offsets[axis], 2)
        mine = grid.block(where)
        other = grid.block(grid.moved(where, "core", 1))
        return mine, other, grid.slot(offsets)

    def gy_loads(step, turn):
        mine, other, _ = blocks_of(step)
        return [
            pltpu.make_async_copy(gy.at[mine, :, : plan.block], gybuf.at[turn, 0], gy_sem.at[turn, 0]),
            pltpu.make_async_copy(gy.at[other, :, : plan.block], gybuf.at[turn, 1], gy_sem.at[turn, 1]),
        ]

    def out_copy(turn, i, block):
        return pltpu.make_async_copy(outbuf.at[turn, i], out_all.at[block], out_sem.at[turn, i])

    for load in gy_loads(0, 0):
        load.start()
    meet(grid.peers(at))
    for part in parts:
        pass_on(part, STEP_ORDER[0])
    n2all[pl.ds(grid.block(at), 1)] = n2x[...][None]

    @pl.loop(0, width // 64)
    def _(i):
        acc[pl.ds(pl.multiple_of(i * 64, 64), 64)] = jnp.zeros((64, 2 * hidden), F32)

    @pl.loop(0, hidden // 64)
    def _(i):
        dw_out[pl.ds(pl.multiple_of(i * 64, 64), 64)] = jnp.zeros((64, width), F32)

    @pl.loop(0, steps)
    def _(step):
        pauses(step, 0)
        mine, other, slot = blocks_of(step)
        turn = lax.rem(step, 2)

        @pl.when(step + 1 < steps)
        def _():
            for load in gy_loads(step + 1, 1 - turn):
                load.start()

        for part in parts:
            ref = n2all.at[other, in_rows[part]]
            remote(ref, ref, gc_send.at[part, 0], gc_recv.at[part, slot], here).wait_recv()
        for load in gy_loads(step, turn):
            load.wait()
        pair = (mine, other)
        normed = jnp.concatenate([n2all[b, :local] for b in pair], axis=0)
        upstream = gybuf[turn].reshape(2 * local, width)
        mixing = jnp.concatenate([tn(n2all[b, local:, :local], pick[...]) for b in pair], axis=0)
        pre = nn(normed, w_in[...])
        gate, up = pre[:, :hidden], pre[:, hidden:]
        sigmoid = jax.nn.sigmoid(gate)
        silu = gate * sigmoid
        act = (silu * up).astype(BF16).astype(F32)
        act_mixed = (act * mixing).astype(BF16)
        pauses(step, 1)

        @pl.when(step >= 2)
        def _():
            for i, block in enumerate(pair):
                out_copy(turn, i, block).wait()

        out = nn(act_mixed, w_out[...]).astype(BF16)
        for i, block in enumerate(pair):
            outbuf[turn, i] = out[i * local : (i + 1) * local]
            out_copy(turn, i, block).start()
        act_grad = nt(upstream, w_out[...])
        choice = nt(pick[...], (act * act_grad).astype(BF16)).astype(BF16)
        act_grad = act_grad * mixing
        gate_grad = act_grad * up * sigmoid * (1.0 + gate * (1.0 - sigmoid))
        pre_grad = jnp.concatenate([gate_grad, act_grad * silu], axis=-1).astype(BF16)
        n2g = nt(pre_grad, w_in[...]).astype(BF16)

        @pl.when(step >= 2)
        def _():
            remote(away.at[turn], core_buf.at[0], c_send.at[turn], c_recv.at[0], partner).wait_send()

        pad = jnp.zeros((MIX_ROWS, width - local), BF16)
        for i, (ref, index) in enumerate(((work, slot), (away, turn))):
            span = slice(i * local, (i + 1) * local)
            ref[index, :local] = n2g[span]
            ref[index, local:] = jnp.concatenate([choice[:, span], pad], axis=-1)
        remote(away.at[turn], core_buf.at[slot], c_send.at[turn], c_recv.at[slot], partner).start()
        pauses(step, 2)
        acc[...] += tn(normed, pre_grad)
        dw_out[...] += tn(act_mixed, upstream)

    pause(3 * steps)
    for turn in range(2):
        for i in range(2):
            out_copy(turn, i, 0).wait()

    @pl.loop(0, width // 64)
    def _(i):
        rows = pl.ds(pl.multiple_of(i * 64, 64), 64)
        dw_in[rows] = acc[rows].astype(BF16)

    for turn in range(2):
        remote(away.at[turn], core_buf.at[0], c_send.at[turn], c_recv.at[0], partner).wait_send()
    for part in parts:
        ref, block = n2all.at[0, in_rows[part]], bufs.at[0, sum_rows[part]]
        for slot in range(steps):
            remote(ref, ref, gc_send.at[part, slot], g_recv.at[part, 0], partner).wait_send()
        for index in range(steps - 1):
            remote(ref, ref, g_send.at[part, index], g_recv.at[part, 0], partner).wait_send()
            remote(block, block, r_send.at[part, index], r_recv.at[part, 0], partner).wait_send()


def fused(plan, n2x, gy, w_in, w_out, pick, collective_id):
    local, width, hidden = plan.local, plan.width, plan.hidden_pad
    steps = len(STEP_ORDER)
    rows = local + MIX_ROWS
    return pl.pallas_call(
        functools.partial(fused_kernel, plan),
        out_shape=(
            jax.ShapeDtypeStruct((rows, width), F32),
            jax.ShapeDtypeStruct((width, 2 * hidden), BF16),
            jax.ShapeDtypeStruct((hidden, width), F32),
            jax.ShapeDtypeStruct((plan.group, local, width), BF16),
        ),
        in_specs=[VMEM, HBM, VMEM, VMEM, VMEM],
        out_specs=(VMEM,) * 3 + (HBM,),
        scratch_shapes=[
            pltpu.VMEM((plan.group, local + MIX_ROWS, width), BF16),
            pltpu.VMEM((2, 2, 2, plan.block, width), BF16),
            pltpu.VMEM((width, 2 * hidden), F32),
            pltpu.VMEM((2, rows, width), BF16),
            pltpu.VMEM((steps, rows, width), BF16),
            pltpu.VMEM((steps, rows, width), BF16),
            pltpu.VMEM((steps - 1, rows, width), BF16),
            pltpu.VMEM((2, 2, local, width), BF16),
            DMA((2, 2)),
            DMA((2, 2)),
            DMA((3, steps - 1)),
            DMA((3, steps)),
            DMA((3, steps)),
            DMA((3, steps)),
            DMA((2,)),
            DMA((steps,)),
            DMA((3, steps - 1)),
            DMA((3, steps - 1)),
        ],
        compiler_params=params(collective_id),
        cost_estimate=busy(100),
        name="fused",
    )(n2x, gy, w_in, w_out, pick)


def turned(value):
    return pltpu.roll(value, 64, 1)


def half_tiles(plan):
    return lax.broadcasted_iota(jnp.int32, (plan.rows, 128), 1) < 64


def column_tiles(plan, pair, gate):
    per = plan.quad // 2
    start = gate * FF + lax.div(pair, per) * (plan.ctx * 64) + lax.rem(pair, per) * 128
    first = lax.div(pair, per) * plan.quad + lax.rem(pair, per) * 2
    return [pl.ds(pl.multiple_of(start + half * plan.quad * 64, 128), 128) for half in range(2)], first


def pack_kernel(plan, both, attn, extra, wq, win):
    low = half_tiles(plan)

    @pl.loop(0, plan.group // 2)
    def _(pair):
        for branch in range(plan.branches):
            made = [[], []]
            for gate in range(2):
                cols, first = column_tiles(plan, pair, gate)
                mine, far = (both[branch, :, col].astype(F32) for col in cols)
                made[0].append(jnp.where(low, mine, turned(far)))
                made[1].append(jnp.where(low, turned(mine), far))
            for i in range(2):
                value = jnp.concatenate(made[i], axis=0).astype(BF16)
                win[pl.ds(first + i, 1), :, branch * 128 : (branch + 1) * 128] = value[None]

    def tile(part, head):
        start = part * HEADS * HEAD_DIM + head // 2 * 128
        return attn[:, start : start + 128].astype(F32)

    def placed(part, head, side):
        value = tile(part, head)
        return value if head % 2 == side else turned(value)

    for member in range(plan.quad):
        heads = [member * 3 + i for i in range(3)]
        for i, head in enumerate(heads):
            value = jnp.where(low, placed(0, head, 0), placed(1, head, 1))
            wq[member, :, i * 128 : (i + 1) * 128] = value.astype(BF16)
        value = jnp.where(low, placed(2, heads[0], 0), placed(2, heads[1], 1))
        wq[member, :, 384:512] = value.astype(BF16)
        value = jnp.where(low, placed(2, heads[2], 0), extra[...].astype(F32))
        wq[member, :, 512:640] = value.astype(BF16)


def pack(plan, both, attn, extra):
    return pl.pallas_call(
        functools.partial(pack_kernel, plan),
        out_shape=(
            jax.ShapeDtypeStruct((plan.quad, plan.rows, plan.wide), BF16),
            jax.ShapeDtypeStruct((plan.group, 2 * plan.rows, plan.hidden_pad), BF16),
        ),
        in_specs=[VMEM] * 3,
        out_specs=(VMEM,) * 2,
        compiler_params=params(),
        cost_estimate=busy(3),
        name="pack",
    )(both, attn, extra)


def unpack_kernel(plan, r_in, r_qkv, r_mix, dw_out, far_out, dense_in, expert_in, attn_in, attn_out, small, dense_out, expert_out):
    low = half_tiles(plan)
    rows = plan.rows

    @pl.loop(0, plan.group // 2)
    def _(pair):
        first = column_tiles(plan, pair, 0)[1]
        for branch in range(plan.branches):
            cols = slice(branch * 128, (branch + 1) * 128)
            sources = [r_in[first + i, :, cols].astype(F32) for i in range(2)]
            for gate in range(2):
                one, two = (value[gate * rows : (gate + 1) * rows] for value in sources)
                places = column_tiles(plan, pair, gate)[0]
                values = jnp.where(low, one, turned(two)), jnp.where(low, turned(one), two)
                for place_at, value in zip(places, values):
                    if branch == 0:
                        dense_in[:, place_at] = value
                    else:
                        expert_in[:, branch - 1, place_at] = value

    def tile(member, number):
        cols = slice(number * 128, (number + 1) * 128)
        return r_qkv[member, :, cols].astype(F32) + r_qkv[plan.quad + member, :, cols].astype(F32)

    def put(part, head, value):
        start = part * HEADS * HEAD_DIM + head // 2 * 128
        attn_in[:, start : start + 128] = value

    for head in range(0, HEADS, 2):
        one, two = (tile((head + i) // 3, (head + i) % 3) for i in range(2))
        put(0, head, jnp.where(low, one, turned(two)))
        put(1, head, jnp.where(low, turned(one), two))
        halves = []
        for i in range(2):
            member, at = divmod(head + i, 3)
            value = tile(member, 3 + at // 2)
            halves.append(value if at % 2 == i else turned(value))
        put(2, head, jnp.where(low, halves[0], halves[1]))
    total = tile(0, 4)
    for member in range(1, plan.quad):
        total = total + tile(member, 4)
    small[...] = total
    mixed = r_mix[0].astype(F32)
    for i in range(1, plan.ctx):
        mixed = mixed + r_mix[i].astype(F32)
    attn_out[...] = mixed
    half = lax.div(lax.axis_index("ctx"), plan.quad)
    for branch in range(plan.branches):
        value = dw_out[branch, pl.ds(half, 1)][0] + far_out[branch].astype(F32)
        if branch == 0:
            dense_out[...] = value
        else:
            expert_out[:, branch - 1, :] = value


def unpack(plan, r_in, r_qkv, r_mix, dw_out, far_out):
    rows, width, own = plan.rows, plan.width, plan.own_hidden
    return pl.pallas_call(
        functools.partial(unpack_kernel, plan),
        out_shape=(
            jax.ShapeDtypeStruct((rows, 2 * FF), F32),
            jax.ShapeDtypeStruct((rows, plan.experts, 2 * FF), F32),
            jax.ShapeDtypeStruct((rows, 3 * HEADS * HEAD_DIM), F32),
            jax.ShapeDtypeStruct((rows, width), F32),
            jax.ShapeDtypeStruct((rows, 128), F32),
            jax.ShapeDtypeStruct((own, width), F32),
            jax.ShapeDtypeStruct((own, plan.experts, width), F32),
        ),
        in_specs=[VMEM] * 5,
        out_specs=(VMEM,) * 7,
        compiler_params=params(),
        cost_estimate=busy(5),
        name="unpack",
    )(r_in, r_qkv, r_mix, dw_out, far_out)


def grid_block(plan, dp, ctx):
    return dp * plan.quad + lax.rem(ctx, plan.quad)


def by_half(half, mine, far, axis):
    return jnp.where(
        half == 0, jnp.stack([mine, far], axis), jnp.stack([far, mine], axis)
    )


def rope_tables(plan):
    half, step = HEAD_DIM // 2, 64
    frequency = np.float32(10000.0) ** (-np.arange(half, dtype=np.float32) / np.float32(half))
    frequency = np.tile(frequency.astype(np.float64), 4)[None]
    coarse = np.arange(0, plan.slots, step)[:, None] * frequency
    fine = np.arange(step)[:, None] * frequency
    sign = np.tile(np.repeat([-1.0, 1.0], half), 2)[None]
    (ca, sa), (cb, sb) = (
        (jnp.asarray(np.cos(a), F32), jnp.asarray(np.sin(a), F32)) for a in (coarse, fine)
    )
    ca, sa, cb, sb = ca[:, None], sa[:, None], cb[None], sb[None]
    cosine = (ca * cb - sa * sb).reshape(plan.slots, 128)
    sine = ((sa * cb + ca * sb) * jnp.asarray(sign, F32)).reshape(plan.slots, 128)
    return cosine, sine


def pick_table(plan):
    table = np.zeros((MIX_ROWS, plan.hidden_pad), np.float32)
    span = HALVES * plan.own_hidden
    for expert in range(plan.experts):
        cols = slice((1 + expert) * span, (2 + expert) * span)
        table[2 + expert, cols] = 1.0
        table[10 + expert, cols] = 1.0
    table[0, :span] = 1.0
    return jnp.asarray(table, BF16)


def pack_qkv(plan, attn_in, attn_gain, ffn_gain, router):
    rows, quad, heads = plan.rows, plan.quad, plan.heads
    qkv = attn_in.reshape(rows, 3, HEADS, HEAD_DIM)
    qkv = jnp.pad(qkv, ((0, 0), (0, 0), (0, quad * heads - HEADS), (0, 0)))
    qkv = qkv.reshape(rows, 3, quad, heads, HEAD_DIM)
    qk = jnp.transpose(qkv[:, :2], (2, 0, 3, 1, 4)).reshape(quad, rows, 2 * plan.head_cols)
    v = jnp.transpose(qkv[:, 2], (1, 0, 2, 3)).reshape(quad, rows, plan.head_cols)
    extra = jnp.concatenate([attn_gain[:, None], ffn_gain[:, None], router], axis=1)
    extra = jnp.pad(extra, ((0, 0), (0, plan.wide - plan.qkv_cols - extra.shape[1])))
    extra = jnp.broadcast_to(extra[None], (quad,) + extra.shape)
    packed = jnp.concatenate([qk, v, extra], axis=-1)
    return jnp.pad(packed, ((0, 0), (0, plan.pad_rows - rows), (0, 0)))


def unpack_qkv(plan, packed):
    rows, quad, heads = plan.rows, plan.quad, plan.heads
    qk = packed[..., : 2 * plan.head_cols].reshape(quad, rows, heads, 2, HEAD_DIM)
    v = packed[..., 2 * plan.head_cols : plan.qkv_cols].reshape(quad, rows, heads, 1, HEAD_DIM)
    qkv = jnp.transpose(jnp.concatenate([qk, v], axis=3), (1, 3, 0, 2, 4))
    qkv = qkv.reshape(rows, 3, quad * heads, HEAD_DIM)[:, :, :HEADS]
    return qkv.reshape(rows, 3 * HEADS * HEAD_DIM)


def pack_in(plan, dense_in, expert_in):
    rows, own = plan.rows, plan.own_hidden
    both = jnp.concatenate([dense_in[:, None], expert_in], axis=1)
    both = both.reshape(rows, plan.branches, 2, plan.dp, HALVES, plan.quad, own)
    both = jnp.transpose(both, (3, 5, 2, 0, 1, 4, 6))
    both = both.reshape(plan.group, 2, rows, plan.hidden)
    pads = ((0, 0), (0, 0), (0, plan.pad_rows - rows), (0, plan.hidden_pad - plan.hidden))
    return jnp.pad(both, pads).reshape(plan.group, 2 * plan.pad_rows, plan.hidden_pad)


def unpack_in(plan, packed):
    rows, own = plan.rows, plan.own_hidden
    both = packed.reshape(plan.group, 2, plan.pad_rows, plan.hidden_pad)
    both = both[:, :, :rows, : plan.hidden]
    both = both.reshape(plan.dp, plan.quad, 2, rows, plan.branches, HALVES, own)
    both = jnp.transpose(both, (3, 4, 2, 0, 5, 1, 6))
    both = both.reshape(rows, plan.branches, 2 * FF).astype(F32)
    return both[:, 0], both[:, 1:]


def shards(
    tokens,
    lengths,
    routes,
    cotangent,
    attn_gain,
    attn_in,
    attn_out,
    ffn_gain,
    router,
    dense_in,
    dense_out,
    expert_in,
    expert_out,
):
    micro, seqs, block, width = tokens.shape
    experts = expert_in.shape[1]
    plan = Plan(lax.axis_size("dp"), lax.axis_size("ctx"), block, width, experts)
    assert micro == HALVES and seqs == 1 and plan.ctx % 4 == 0 and plan.dp % 2 == 0
    quad, local = plan.quad, plan.local
    dp, ctx = place()
    half, member = lax.div(ctx, quad), lax.rem(ctx, quad)
    across = [(i, (i + quad) % plan.ctx) for i in range(plan.ctx)]

    def swap(value):
        return lax.ppermute(value, "ctx", across)

    def pick_mine(value):
        return lax.dynamic_index_in_dim(value, half, 0, keepdims=False)

    def pick_far(value):
        return lax.dynamic_index_in_dim(value, 1 - half, 0, keepdims=False)

    slot = ctx * block + jnp.arange(block, dtype=jnp.int32)
    valid = (slot[None] < lengths).astype(BF16)
    grad_all = cotangent[:, 0] * valid[..., None]
    tail = round_up(plan.rows + 2, 16)
    route_rows = jnp.transpose(routes[:, 0], (0, 2, 1)).astype(BF16)
    route_rows = jnp.pad(route_rows, ((0, 0), (0, tail - plan.rows - 2), (0, width - block)))
    length = pick_mine(lengths)
    out_own = jnp.concatenate([dense_out[:, None], expert_out], axis=1)
    out_own = jnp.transpose(out_own, (1, 0, 2))
    out_far = swap(out_own)
    gyw = jnp.concatenate(
        [grad_all, jnp.broadcast_to(attn_out, (2,) + attn_out.shape), route_rows], axis=1
    )

    if plan.tiled:
        both = jnp.concatenate([dense_in[None], jnp.transpose(expert_in, (1, 0, 2))])
        extra = jnp.concatenate([attn_gain[:, None], ffn_gain[:, None], router], axis=1)
        extra = jnp.pad(extra, ((0, 0), (64, 64 - extra.shape[1])))
        wq, win = pack(plan, both, attn_in, extra)
    else:
        wq = pack_qkv(plan, attn_in, attn_gain, ffn_gain, router)
        win = pack_in(plan, dense_in, expert_in)

    cosine, sine = rope_tables(plan)
    xs, w_seq, normed_seq, qk, v, lse, mixed, gy, w_in, gysrc, *owned = front(
        plan,
        length,
        tokens[:, 0],
        wq,
        win,
        gyw,
        cosine,
        sine,
        1,
    )
    x_seq = xs.reshape(plan.slots, width)
    if plan.tiled:
        n2x, middle, gates, w_mix = owned
    else:
        extra = w_seq[:, plan.qkv_cols :]
        gain_one = extra[:, 0].astype(F32)[None]
        gain_two = extra[:, 1].astype(F32)[None]
        w_route = extra[:, 2 : 2 + experts]
        mixed = jnp.transpose(mixed, (1, 2, 0, 3)).reshape(local, quad * plan.head_cols)[:, :width]
        w_mix = gy[:, :, block : block + plan.rows].reshape(plan.dp, quad, 2, plan.rows, width)
        w_mix = by_half(half, w_mix[:, :, 0], w_mix[:, :, 1], 1).reshape(width, width)

        x = jnp.stack(
            [
                lax.dynamic_index_in_dim(xs, ctx, 0, keepdims=False),
                lax.dynamic_index_in_dim(xs, (1 - half) * quad + member, 0, keepdims=False),
            ]
        )
        x = x.reshape(local, width).astype(F32)
        middle = x + nn(mixed, w_mix)
        inverse_two = lax.rsqrt(jnp.mean(middle * middle, axis=-1, keepdims=True) + EPSILON)
        normed_two = (middle * inverse_two * gain_two).astype(BF16)
        own = lax.dynamic_index_in_dim(gy, grid_block(plan, dp, ctx), 0, keepdims=False)
        grad_y = own[:, :block].reshape(local, width)
        route_local = own[:, block + plan.rows : block + plan.rows + 2, :block]
        route_local = jnp.transpose(route_local, (0, 2, 1)).reshape(local, 2)
        logits = nn(normed_two, w_route)
        choose = (route_local[..., None] == jnp.arange(experts, dtype=BF16)).astype(F32)
        picked = jnp.sum(choose * logits[:, None, :], axis=-1)
        gates = jax.nn.softmax(picked, axis=-1)
        mixing = jnp.sum(gates[..., None] * choose, axis=1)
        mixing_t = mixing.T
        mixing_high = mixing_t.astype(BF16)
        mixing_low = (mixing_t - mixing_high.astype(F32)).astype(BF16)
        pads = ((2, 6 - experts), (0, 0))
        mix_rows = jnp.concatenate([jnp.pad(mixing_high, pads), jnp.pad(mixing_low, pads)])
        mix_rows = mix_rows.at[0].set(1.0)
        mix_rows = jnp.pad(mix_rows, ((0, 0), (0, width - local)))
        n2x = jnp.concatenate([normed_two, mix_rows])

    w_out = by_half(half, out_own, out_far, 1).reshape(plan.hidden, width)
    w_out = jnp.pad(w_out, ((0, plan.hidden_pad - plan.hidden), (0, 0)))
    if plan.dp == 4 and quad == 4:
        n2g_sum, dw_in, dw_out, out_part = fused(plan, n2x, gy, w_in, w_out, pick_table(plan), 3)
    else:
        n2x = gather(plan, n2x, 3)
        out_part, n2g_part, dw_in, dw_out = ffn(plan, n2x, gy, w_in, w_out, pick_table(plan))
        n2g_sum = reduce(plan, n2g_part, 5)
        out_part = reduce(plan, out_part, 7)

    if plan.tiled:
        given = (n2g_sum, gates, n2x, gysrc, w_mix, mixed)
    else:
        normed_two_grad = n2g_sum[:local]
        mixing_grad = n2g_sum[local + 2 : local + 2 + experts, :local].T
        choice_grad = jnp.sum(choose * mixing_grad[:, None, :], axis=-1)
        pick_grad = gates * (choice_grad - jnp.sum(gates * choice_grad, axis=-1, keepdims=True))
        logit_grad = jnp.sum(pick_grad[..., None] * choose, axis=1).astype(BF16)
        router_grad = tn(normed_two, logit_grad)
        normed_two_grad = normed_two_grad + nt(logit_grad, w_route)
        gain_two_grad = jnp.sum(normed_two_grad * middle * inverse_two, axis=0)
        scaled = normed_two_grad * gain_two
        middle_grad = (
            grad_y.astype(F32)
            + inverse_two * scaled
            - middle * inverse_two**3 * jnp.mean(scaled * middle, axis=-1, keepdims=True)
        )
        attn_grad = middle_grad.astype(BF16)
        dw_mix = tn(mixed, attn_grad).astype(BF16).reshape(plan.dp, plan.ctx, plan.rows, width)
        mixed_grad = nt(attn_grad, w_mix).astype(BF16)
        mixed_grad = jnp.pad(mixed_grad, ((0, 0), (0, quad * plan.head_cols - width)))
        mixed_grad = mixed_grad.reshape(2, block, quad, plan.head_cols)
        first = plan.qkv_cols - (plan.wide - 128)
        small = jnp.concatenate([gain_two_grad[:, None], router_grad], axis=1)
        small = jnp.pad(small, ((0, 0), (first + 1, 127 - first - small.shape[1])))
        given = (jnp.transpose(mixed_grad, (2, 0, 1, 3)), dw_mix, small, middle_grad)
    dw_out = dw_out[: plan.hidden].reshape(plan.branches, HALVES, plan.own_hidden, width)
    r_qkv, r_mix, r_in, far_out, activations, input_grad = back(
        plan,
        length,
        x_seq,
        w_seq,
        cosine,
        sine,
        normed_seq,
        qk,
        v,
        lse,
        dw_in.astype(BF16).reshape(plan.dp * HALVES, quad * plan.rows, 2 * plan.hidden_pad),
        dw_out,
        out_part,
        middle,
        given,
        4,
    )

    if plan.tiled:
        dense_in_grad, expert_in_grad, attn_in_grad, attn_out_grad, small, dense_out_grad, expert_out_grad = unpack(
            plan, r_in, r_qkv, r_mix, dw_out, far_out
        )
        small = small[:, 64 : 66 + experts]
    else:
        r_qkv = r_qkv[:, : plan.rows].astype(F32).reshape(HALVES, quad, plan.rows, plan.wide)
        r_qkv = jnp.sum(r_qkv, axis=0)
        attn_in_grad = unpack_qkv(plan, r_qkv)
        small = jnp.sum(r_qkv[:, :, plan.qkv_cols :], axis=0)
        attn_out_grad = jnp.sum(r_mix.astype(F32), axis=0)
        dense_in_grad, expert_in_grad = unpack_in(plan, r_in)
        dw_out = pick_mine(jnp.moveaxis(dw_out, 1, 0)) + far_out.astype(F32)
        dense_out_grad, expert_out_grad = dw_out[0], jnp.transpose(dw_out[1:], (1, 0, 2))
    return (
        activations[:, None],
        input_grad[:, None],
        small[:, 0],
        attn_in_grad,
        attn_out_grad,
        small[:, 1],
        small[:, 2 : 2 + experts],
        dense_in_grad,
        dense_out_grad,
        expert_in_grad,
        expert_out_grad,
    )


def solution(mesh):
    rows = P(("dp", "ctx"))
    matrix = P(("dp", "ctx"), None)
    cube = P(("dp", "ctx"), None, None)
    slots = P(None, "dp", "ctx", None)
    in_specs = (
        slots,
        P(None, "dp"),
        slots,
        slots,
        rows,
        matrix,
        matrix,
        rows,
        matrix,
        matrix,
        matrix,
        cube,
        cube,
    )
    out_specs = (
        slots,
        slots,
        rows,
        matrix,
        matrix,
        rows,
        matrix,
        matrix,
        matrix,
        cube,
        cube,
    )
    return jax.shard_map(shards, mesh=mesh, in_specs=in_specs, out_specs=out_specs, check_vma=False)
```

profile of v0, /device:TPU:0, one launch (start us, length us, event | category | flops | bytes accessed | tf_op | source)
XLA Modules:
  0.0 329.5 jit_solution(8419322770352888355)
XLA Ops:
  0.7 1.1 copy.52
  1.9 1.0 fusion.2
  2.8 4.1 %collective-permute-start = (bf16[5,64,768]{2,1,0:T(8,128)(2,1)S(1)}, bf16[5,64,768]{2,1,0:T(8,128)(2,1)S(1)}, u32[]{:S(2)}, u32[]{:S(2)}) collective-permute-start(bf16[5,64,768]{2,1,0:T(8,128)(2,1)S(1)} %get-tuple-element.113), channel_id=1, source_target_pairs={{0,4},{1,5},{2,6},{3,7},{4,0},{5,1},{6,2},{7,3},{8,12},{9,13},{10,... | collective-permute-start | bytes 1474568 | tf_op jit(solution)/shard_map/ppermute | solution.py:1969
  6.9 0.0 copy-done.10
  6.9 0.0 copy-done.12
  7.0 0.1 copy.50
  7.1 0.4 copy.58
  7.5 0.6 constant_dynamic-slice_fusion
  8.1 0.1 compare_convert_fusion
  8.2 0.7 pad.8.extra
  8.9 0.1 bitcast_multiply_fusion.1
  9.0 0.0 copy-start.5
  9.0 0.0 copy-start.6
  9.0 0.0 copy-start.7
  9.0 0.0 copy-start.8
  9.0 2.0 pad_maximum_fusion.both
  11.0 0.8 fusion.1.gyw
  11.9 3.2 pack.1
  15.1 0.9 multiply_add_fusion
  16.0 0.9 bitcast_multiply_fusion.sine
  16.8 105.2 %front.1 = (bf16[8,128,768]{2,1,0:T(8,128)(2,1)}, bf16[768,640]{1,0:T(8,128)(2,1)}, bf16[1024,768]{1,0:T(8,128)(2,1)}, bf16[1024,384]{1,0:T(8,128)(2,1)}, bf16[1...) custom-call(s32[1]{0:T(128)} %bitcast.length_ref, ...), custom_call_target="tpu_custom_call" | custom-call | bytes 306000000 | tf_op jit(solution)/shard_map/front/pallas_call | solution.py:763
  122.1 0.0 collective-permute-done
  122.1 0.2 maximum_select_fusion
  122.2 1.0 copy.53
  123.3 82.1 %fused.1 = (f32[272,768]{1,0:T(8,128)}, bf16[768,1280]{1,0:T(8,128)(2,1)}, f32[640,768]{1,0:T(8,128)}, bf16[16,256,768]{2,1,0:T(8,128)(2,1)}) custom-call(bf16[272,768]{1,0:T(8,128)(2,1)} %get-tuple-element.52.n2x.rest_2_, bf16[16,2,160,768]{3,2,1,0:T(8,128)(2,1)} %get-tuple-element.53.gy, bf16[768,1280]{1,0:T(8,128)(2,1)} %get-tuple-element.54.w_in, ...), custom_call_target="tpu_custom_call" | custom-call | bytes 340000000 | tf_op jit(solution)/shard_map/fused/pallas_call | solution.py:1687
  205.4 113.6 %back.1 = (bf16[8,24,640]{2,1,0:T(8,128)(2,1)}, bf16[8,24,768]{2,1,0:T(8,128)(2,1)}, bf16[16,48,640]{2,1,0:T(8,128)(2,1)}, bf16[5,64,768]{2,1,0:T(8,128)(2,1)}, ...) custom-call(s32[1]{0:T(128)} %bitcast.length_ref, bf16[1024,768]{1,0:T(8,128)(2,1)} %bitcast.46, ...), custom_call_target="tpu_custom_call" | custom-call | bytes 306000000 | tf_op jit(solution)/shard_map/back/pallas_call | solution.py:1303
  319.0 6.0 %unpack.1 = (f32[24,4096]{1,0:T(8,128)}, f32[24,4,4096]{2,1,0:T(4,128)}, f32[24,2304]{1,0:T(8,128)}, f32[24,768]{1,0:T(8,128)}, f32[24,128]{1,0:T(8,128)}, /*index=5*/f32[64,768]{1,0:T(8,128)}, f32[64,4,768]{2,1,0:T(4,128)}) custom-call(bf16[16,48,640]{2,1,0:T(8,128)(2,1)} %get-tuple-element.66.r_in, bf16[8,24,640]{2,1,0:T(8,128)(2,1)} %get-tuple-element.67.r_qkv, ...), custom_call_target="tpu_custom_call" | custom-call | bytes 17000000 | tf_op jit(solution)/shard_map/unpack/pallas_call | solution.py:1845
  325.0 1.5 slice_reduce_fusion
  326.5 0.8 slice.15
  327.3 0.7 copy.56
  328.0 0.7 copy.61
  328.7 0.7 copy.62
  (28 shorter events, 0.1 us)
Async XLA Ops:
  0.6 6.3 %copy-start.9 = (s32[2,1,128,2]{2,3,1,0:T(2,128)S(1)}, s32[2,1,128,2]{2,3,1,0:T(2,128)}, u32[]{:S(2)}) copy-start(s32[2,1,128,2]{2,3,1,0:T(2,128)} %param.21) | copy-start | bytes 6148
  0.7 6.3 %copy-start.10 = (bf16[24,4]{0,1:T(4,128)(2,1)S(1)}, bf16[24,4]{0,1:T(4,128)(2,1)}, u32[]{:S(2)}) copy-start(bf16[24,4]{0,1:T(4,128)(2,1)} %param.27) | copy-start | bytes 580
  0.7 6.3 %copy-start.12 = (bf16[24]{0:T(256)(128)(2,1)S(1)}, bf16[24]{0:T(256)(128)(2,1)}, u32[]{:S(2)}) copy-start(bf16[24]{0:T(256)(128)(2,1)} %param.26) | copy-start | bytes 148
  0.7 6.3 %copy-start.13 = (bf16[24]{0:T(256)(128)(2,1)S(1)}, bf16[24]{0:T(256)(128)(2,1)}, u32[]{:S(2)}) copy-start(bf16[24]{0:T(256)(128)(2,1)} %param.23) | copy-start | bytes 148
  0.7 6.4 %copy-start = (bf16[24,4,4096]{2,1,0:T(4,128)(2,1)S(1)}, bf16[24,4,4096]{2,1,0:T(4,128)(2,1)}, u32[]{:S(2)}) copy-start(bf16[24,4,4096]{2,1,0:T(4,128)(2,1)} %param.30) | copy-start | bytes 2359300
  0.7 6.8 %copy-start.14 = (s32[2,1]{0,1:T(1,128)S(1)}, s32[2,1]{0,1:T(1,128)}, u32[]{:S(2)}) copy-start(s32[2,1]{0,1:T(1,128)} %param.20) | copy-start | bytes 28
  0.7 8.2 %copy-start.3 = (bf16[2,1,128,768]{3,2,1,0:T(8,128)(2,1)S(1)}, bf16[2,1,128,768]{3,2,1,0:T(8,128)(2,1)}, u32[]{:S(2)}) copy-start(bf16[2,1,128,768]{3,2,1,0:T(8,128)(2,1)} %param.22) | copy-start | bytes 1179652
  2.8 119.2 %collective-permute-start = (bf16[5,64,768]{2,1,0:T(8,128)(2,1)S(1)}, bf16[5,64,768]{2,1,0:T(8,128)(2,1)S(1)}, u32[]{:S(2)}, u32[]{:S(2)}) collective-permute-start(bf16[5,64,768]{2,1,0:T(8,128)(2,1)S(1)} %get-tuple-element.113), channel_id=1, source_target_pairs={{0,4},{1,5},{2,6},{3,7},{4,0},{5,1},{6,2},{7,3},{8,12},{9,13},{10,... | collective-permute-start | bytes 1474568 | tf_op jit(solution)/shard_map/ppermute | solution.py:1969
  7.1 3.9 %copy-start.4 = (bf16[24,768]{1,0:T(8,128)(2,1)S(1)}, bf16[24,768]{1,0:T(8,128)(2,1)}, u32[]{:S(2)}) copy-start(bf16[24,768]{1,0:T(8,128)(2,1)} %param.25) | copy-start | bytes 110596
  9.0 6.1 %copy-start.5 = (f32[64,128]{1,0:T(8,128)S(1)}, f32[64,128]{1,0:T(8,128)}, u32[]{:S(2)}) copy-start(f32[64,128]{1,0:T(8,128)} %constant.33.clone) | copy-start | bytes 98308
  9.0 6.0 %copy-start.6 = (f32[64,128]{1,0:T(8,128)S(1)}, f32[64,128]{1,0:T(8,128)}, u32[]{:S(2)}) copy-start(f32[64,128]{1,0:T(8,128)} %constant.32.clone) | copy-start | bytes 98308
  9.0 6.0 %copy-start.7 = (f32[16,128]{1,0:T(8,128)S(1)}, f32[16,128]{1,0:T(8,128)}, u32[]{:S(2)}) copy-start(f32[16,128]{1,0:T(8,128)} %constant.31.clone) | copy-start | bytes 24580
  9.0 6.0 %copy-start.8 = (f32[16,128]{1,0:T(8,128)S(1)}, f32[16,128]{1,0:T(8,128)}, u32[]{:S(2)}) copy-start(f32[16,128]{1,0:T(8,128)} %constant.30.clone) | copy-start | bytes 24580
  11.0 5.0 %copy-start.11 = (f32[128]{0:T(128)S(1)}, f32[128]{0:T(128)}, u32[]{:S(2)}) copy-start(f32[128]{0:T(128)} %constant.51) | copy-start | bytes 1540
  319.0 9.0 %copy-start.2 = (bf16[2,128,768]{2,1,0:T(8,128)(2,1)S(1)}, bf16[2,128,768]{2,1,0:T(8,128)(2,1)}, u32[]{:S(2)}) copy-start(bf16[2,128,768]{2,1,0:T(8,128)(2,1)} %get-tuple-element.64) | copy-start | bytes 1179652
  319.0 9.7 %copy-start.1 = (bf16[2,128,768]{2,1,0:T(8,128)(2,1)S(1)}, bf16[2,128,768]{2,1,0:T(8,128)(2,1)}, u32[]{:S(2)}) copy-start(bf16[2,128,768]{2,1,0:T(8,128)(2,1)} %get-tuple-element.65) | copy-start | bytes 1179652
where the time goes:
time: 330 us; the launch traced here: 329 us
  Pallas kernels  310 us (94%)
  local copies, waits for them, and re-layouts  8.42 us (3%)
  other arithmetic  5.92 us (2%)
  starting transfers between devices  4.1 us (1%)
    pallas_call x1, Pallas kernels, back(): pl.pallas_call(functools.partial(back_kernel, plan, summed), out_shape=(j...  114 us
    pallas_call x1, Pallas kernels, front(): pl.pallas_call(functools.partial(front_kernel, plan), out_shape=(jax.Shap...  105 us
    pallas_call x1, Pallas kernels, fused(): pl.pallas_call(functools.partial(fused_kernel, plan), out_shape=(jax.Shap...  82.1 us
  transfers between devices with their start and end apart: 1, of which 0 were waited for; matrix products, arithmetic and copies ran while one was open for 2% of the time, Pallas kernels for 33%

commit v1 on v0

--- a/solution.py
+++ b/solution.py
@@ -1785,7 +1785,9 @@
     )(both, attn, extra)
 
 
-def unpack_kernel(plan, r_in, r_qkv, r_mix, dw_out, far_out, dense_in, expert_in, attn_in, attn_out, small, dense_out, expert_out):
+def unpack_kernel(plan, r_in, r_qkv, r_mix, dw_out, far_out, act, grad, dense_in, expert_in, attn_in, attn_out, gain_one, gain_two, router, dense_out, expert_out, act_out, grad_out):
+    act_out[...] = act[...]
+    grad_out[...] = grad[...]
     low = half_tiles(plan)
     rows = plan.rows
 
@@ -1826,7 +1828,10 @@
     total = tile(0, 4)
     for member in range(1, plan.quad):
         total = total + tile(member, 4)
-    small[...] = total
+    columns = jnp.transpose(jnp.concatenate([total] * 2, axis=0)[:32], (1, 0))
+    gain_one[...] = columns[64:72, :rows][:1]
+    gain_two[...] = columns[64:72, :rows][1:2]
+    router[...] = total[:, 66 : 66 + plan.experts]
     mixed = r_mix[0].astype(F32)
     for i in range(1, plan.ctx):
         mixed = mixed + r_mix[i].astype(F32)
@@ -1840,7 +1845,7 @@
             expert_out[:, branch - 1, :] = value
 
 
-def unpack(plan, r_in, r_qkv, r_mix, dw_out, far_out):
+def unpack(plan, r_in, r_qkv, r_mix, dw_out, far_out, act, grad):
     rows, width, own = plan.rows, plan.width, plan.own_hidden
     return pl.pallas_call(
         functools.partial(unpack_kernel, plan),
@@ -1849,16 +1854,20 @@
             jax.ShapeDtypeStruct((rows, plan.experts, 2 * FF), F32),
             jax.ShapeDtypeStruct((rows, 3 * HEADS * HEAD_DIM), F32),
             jax.ShapeDtypeStruct((rows, width), F32),
-            jax.ShapeDtypeStruct((rows, 128), F32),
+            jax.ShapeDtypeStruct((1, rows), F32),
+            jax.ShapeDtypeStruct((1, rows), F32),
+            jax.ShapeDtypeStruct((rows, plan.experts), F32),
             jax.ShapeDtypeStruct((own, width), F32),
             jax.ShapeDtypeStruct((own, plan.experts, width), F32),
+            jax.ShapeDtypeStruct(act.shape, BF16),
+            jax.ShapeDtypeStruct(grad.shape, BF16),
         ),
-        in_specs=[VMEM] * 5,
-        out_specs=(VMEM,) * 7,
+        in_specs=[VMEM] * 7,
+        out_specs=(VMEM,) * 11,
         compiler_params=params(),
         cost_estimate=busy(5),
         name="unpack",
-    )(r_in, r_qkv, r_mix, dw_out, far_out)
+    )(r_in, r_qkv, r_mix, dw_out, far_out, act, grad)
 
 
 def grid_block(plan, dp, ctx):
@@ -2106,27 +2115,28 @@
     )
 
     if plan.tiled:
-        dense_in_grad, expert_in_grad, attn_in_grad, attn_out_grad, small, dense_out_grad, expert_out_grad = unpack(
-            plan, r_in, r_qkv, r_mix, dw_out, far_out
-        )
-        small = small[:, 64 : 66 + experts]
+        results = unpack(plan, r_in, r_qkv, r_mix, dw_out, far_out, activations, input_grad)
+        dense_in_grad, expert_in_grad, attn_in_grad, attn_out_grad = results[:4]
+        gain_one_grad, gain_two_grad, router_grad = results[4].reshape(-1), results[5].reshape(-1), results[6]
+        dense_out_grad, expert_out_grad, activations, input_grad = results[7:]
     else:
         r_qkv = r_qkv[:, : plan.rows].astype(F32).reshape(HALVES, quad, plan.rows, plan.wide)
         r_qkv = jnp.sum(r_qkv, axis=0)
         attn_in_grad = unpack_qkv(plan, r_qkv)
         small = jnp.sum(r_qkv[:, :, plan.qkv_cols :], axis=0)
         attn_out_grad = jnp.sum(r_mix.astype(F32), axis=0)
+        gain_one_grad, gain_two_grad, router_grad = small[:, 0], small[:, 1], small[:, 2 : 2 + experts]
         dense_in_grad, expert_in_grad = unpack_in(plan, r_in)
         dw_out = pick_mine(jnp.moveaxis(dw_out, 1, 0)) + far_out.astype(F32)
         dense_out_grad, expert_out_grad = dw_out[0], jnp.transpose(dw_out[1:], (1, 0, 2))
     return (
         activations[:, None],
         input_grad[:, None],
-        small[:, 0],
+        gain_one_grad,
         attn_in_grad,
         attn_out_grad,
-        small[:, 1],
-        small[:, 2 : 2 + experts],
+        gain_two_grad,
+        router_grad,
         dense_in_grad,
         dense_out_grad,
         expert_in_grad,

time: 330 us -> 327 us (level)
  no operation moved by 1% of the time
where the time goes in v1:
time: 327 us
  Pallas kernels  310 us (95%)
  other arithmetic  5.93 us (2%)
  local copies, waits for them, and re-layouts  5.37 us (2%)
  starting transfers between devices  4.1 us (1%)
    pallas_call x1, Pallas kernels, back(): pl.pallas_call(functools.partial(back_kernel, plan, summed), out_shape=(j...  114 us
    pallas_call x1, Pallas kernels, front(): pl.pallas_call(functools.partial(front_kernel, plan), out_shape=(jax.Shap...  105 us
    pallas_call x1, Pallas kernels, fused(): pl.pallas_call(functools.partial(fused_kernel, plan), out_shape=(jax.Shap...  82.1 us
  transfers between devices with their start and end apart: 1, of which 0 were waited for; matrix products, arithmetic and copies ran while one was open for 2% of the time, Pallas kernels for 33%

profile of v1, /device:TPU:0, one launch (start us, length us, event | category | flops | bytes accessed | tf_op | source)
XLA Modules:
  0.0 326.7 jit_solution(17959171761762446188)
XLA Ops:
  0.7 1.1 copy.52
  1.9 1.0 fusion.2
  2.8 4.1 %collective-permute-start = (bf16[5,64,768]{2,1,0:T(8,128)(2,1)S(1)}, bf16[5,64,768]{2,1,0:T(8,128)(2,1)S(1)}, u32[]{:S(2)}, u32[]{:S(2)}) collective-permute-start(bf16[5,64,768]{2,1,0:T(8,128)(2,1)S(1)} %get-tuple-element.119), channel_id=1, source_target_pairs={{0,4},{1,5},{2,6},{3,7},{4,0},{5,1},{6,2},{7,3},{8,12},{9,13},{10,... | collective-permute-start | bytes 1474568 | tf_op jit(solution)/shard_map/ppermute | solution.py:1978
  6.9 0.0 copy-done.7
  6.9 0.0 copy-done.8
  6.9 0.0 copy-done.10
  6.9 0.0 copy-done.11
  7.0 0.1 copy.50
  7.1 0.0 copy-done
  7.1 0.4 copy.58
  7.5 0.6 constant_dynamic-slice_fusion
  8.1 0.1 compare_convert_fusion
  8.2 0.7 pad.8.extra
  8.9 0.1 bitcast_multiply_fusion.1
  9.0 0.0 copy-start.3
  9.0 0.0 copy-start.4
  9.0 0.0 copy-start.5
  9.0 0.0 copy-start.6
  9.0 2.0 pad_maximum_fusion.both
  11.0 0.0 copy-done.2
  11.0 0.8 fusion.1.gyw
  11.9 3.2 pack.1
  15.0 0.9 multiply_add_fusion
  16.0 0.9 bitcast_multiply_fusion.sine
  16.8 105.2 %front.1 = (bf16[8,128,768]{2,1,0:T(8,128)(2,1)}, bf16[768,640]{1,0:T(8,128)(2,1)}, bf16[1024,768]{1,0:T(8,128)(2,1)}, bf16[1024,384]{1,0:T(8,128)(2,1)}, bf16[1...) custom-call(s32[1]{0:T(128)} %bitcast.length_ref, ...), custom_call_target="tpu_custom_call" | custom-call | bytes 306000000 | tf_op jit(solution)/shard_map/front/pallas_call | solution.py:763
  122.1 0.0 collective-permute-done
  122.1 0.2 maximum_select_fusion
  122.2 1.0 copy.53
  123.3 82.1 %fused.1 = (f32[272,768]{1,0:T(8,128)}, bf16[768,1280]{1,0:T(8,128)(2,1)}, f32[640,768]{1,0:T(8,128)}, bf16[16,256,768]{2,1,0:T(8,128)(2,1)}) custom-call(bf16[272,768]{1,0:T(8,128)(2,1)} %get-tuple-element.56.n2x.rest_2_, bf16[16,2,160,768]{3,2,1,0:T(8,128)(2,1)} %get-tuple-element.57.gy, bf16[768,1280]{1,0:T(8,128)(2,1)} %get-tuple-element.58.w_in, ...), custom_call_target="tpu_custom_call" | custom-call | bytes 340000000 | tf_op jit(solution)/shard_map/fused/pallas_call | solution.py:1687
  205.4 113.6 %back.1 = (bf16[8,24,640]{2,1,0:T(8,128)(2,1)}, bf16[8,24,768]{2,1,0:T(8,128)(2,1)}, bf16[16,48,640]{2,1,0:T(8,128)(2,1)}, bf16[5,64,768]{2,1,0:T(8,128)(2,1)}, ...) custom-call(s32[1]{0:T(128)} %bitcast.length_ref, bf16[1024,768]{1,0:T(8,128)(2,1)} %bitcast.48, ...), custom_call_target="tpu_custom_call" | custom-call | bytes 306000000 | tf_op jit(solution)/shard_map/back/pallas_call | solution.py:1303
  319.0 6.3 %unpack.1 = (f32[24,4096]{1,0:T(8,128)}, f32[24,4,4096]{2,1,0:T(4,128)}, f32[24,2304]{1,0:T(8,128)}, f32[24,768]{1,0:T(8,128)}, f32[1,24]{1,0:T(1,128)}, /*index...) custom-call(bf16[16,48,640]{2,1,0:T(8,128)(2,1)} %get-tuple-element., ...), custom_call_target="tpu_custom_call" | custom-call | bytes 17000000 | tf_op jit(solution)/shard_map/unpack/pallas_call | solution.py:1850
  325.3 1.4 copy.56
  (20 shorter events, 0.1 us)
Async XLA Ops:
  0.6 6.3 %copy-start.7 = (s32[2,1,128,2]{2,3,1,0:T(2,128)S(1)}, s32[2,1,128,2]{2,3,1,0:T(2,128)}, u32[]{:S(2)}) copy-start(s32[2,1,128,2]{2,3,1,0:T(2,128)} %param.21) | copy-start | bytes 6148
  0.7 6.3 %copy-start.8 = (bf16[24,4]{0,1:T(4,128)(2,1)S(1)}, bf16[24,4]{0,1:T(4,128)(2,1)}, u32[]{:S(2)}) copy-start(bf16[24,4]{0,1:T(4,128)(2,1)} %param.27) | copy-start | bytes 580
  0.7 6.3 %copy-start.10 = (bf16[24]{0:T(256)(128)(2,1)S(1)}, bf16[24]{0:T(256)(128)(2,1)}, u32[]{:S(2)}) copy-start(bf16[24]{0:T(256)(128)(2,1)} %param.26) | copy-start | bytes 148
  0.7 6.3 %copy-start.11 = (bf16[24]{0:T(256)(128)(2,1)S(1)}, bf16[24]{0:T(256)(128)(2,1)}, u32[]{:S(2)}) copy-start(bf16[24]{0:T(256)(128)(2,1)} %param.23) | copy-start | bytes 148
  0.7 6.4 %copy-start = (bf16[24,4,4096]{2,1,0:T(4,128)(2,1)S(1)}, bf16[24,4,4096]{2,1,0:T(4,128)(2,1)}, u32[]{:S(2)}) copy-start(bf16[24,4,4096]{2,1,0:T(4,128)(2,1)} %param.30) | copy-start | bytes 2359300
  0.7 6.8 %copy-start.12 = (s32[2,1]{0,1:T(1,128)S(1)}, s32[2,1]{0,1:T(1,128)}, u32[]{:S(2)}) copy-start(s32[2,1]{0,1:T(1,128)} %param.20) | copy-start | bytes 28
  0.7 8.2 %copy-start.1 = (bf16[2,1,128,768]{3,2,1,0:T(8,128)(2,1)S(1)}, bf16[2,1,128,768]{3,2,1,0:T(8,128)(2,1)}, u32[]{:S(2)}) copy-start(bf16[2,1,128,768]{3,2,1,0:T(8,128)(2,1)} %param.22) | copy-start | bytes 1179652
  2.8 119.2 %collective-permute-start = (bf16[5,64,768]{2,1,0:T(8,128)(2,1)S(1)}, bf16[5,64,768]{2,1,0:T(8,128)(2,1)S(1)}, u32[]{:S(2)}, u32[]{:S(2)}) collective-permute-start(bf16[5,64,768]{2,1,0:T(8,128)(2,1)S(1)} %get-tuple-element.119), channel_id=1, source_target_pairs={{0,4},{1,5},{2,6},{3,7},{4,0},{5,1},{6,2},{7,3},{8,12},{9,13},{10,... | collective-permute-start | bytes 1474568 | tf_op jit(solution)/shard_map/ppermute | solution.py:1978
  7.1 3.9 %copy-start.2 = (bf16[24,768]{1,0:T(8,128)(2,1)S(1)}, bf16[24,768]{1,0:T(8,128)(2,1)}, u32[]{:S(2)}) copy-start(bf16[24,768]{1,0:T(8,128)(2,1)} %param.25) | copy-start | bytes 110596
  9.0 6.1 %copy-start.3 = (f32[64,128]{1,0:T(8,128)S(1)}, f32[64,128]{1,0:T(8,128)}, u32[]{:S(2)}) copy-start(f32[64,128]{1,0:T(8,128)} %constant.33.clone) | copy-start | bytes 98308
  9.0 6.0 %copy-start.4 = (f32[64,128]{1,0:T(8,128)S(1)}, f32[64,128]{1,0:T(8,128)}, u32[]{:S(2)}) copy-start(f32[64,128]{1,0:T(8,128)} %constant.32.clone) | copy-start | bytes 98308
  9.0 6.0 %copy-start.5 = (f32[16,128]{1,0:T(8,128)S(1)}, f32[16,128]{1,0:T(8,128)}, u32[]{:S(2)}) copy-start(f32[16,128]{1,0:T(8,128)} %constant.31.clone) | copy-start | bytes 24580
  9.0 6.0 %copy-start.6 = (f32[16,128]{1,0:T(8,128)S(1)}, f32[16,128]{1,0:T(8,128)}, u32[]{:S(2)}) copy-start(f32[16,128]{1,0:T(8,128)} %constant.30.clone) | copy-start | bytes 24580
  11.0 5.0 %copy-start.9 = (f32[128]{0:T(128)S(1)}, f32[128]{0:T(128)}, u32[]{:S(2)}) copy-start(f32[128]{0:T(128)} %constant.51) | copy-start | bytes 1540

commit v2 on v1

--- a/solution.py
+++ b/solution.py
@@ -891,7 +891,8 @@
 
 
 class Fold:
-    def __init__(self, plan, src, dst, core_buf, y_buf, added, sems):
+    def __init__(self, plan, src, dst, core_buf, y_buf, added, sems, quad_refs=()):
+        self.quad_refs = quad_refs
         self.plan, self.src, self.dst = plan, src, dst
         self.core_buf, self.y_buf, self.added = core_buf, y_buf, added
         self.core_send, self.core_recv, self.y_send, self.y_recv, self.send, self.recv = sems
@@ -970,11 +971,59 @@
                 total = total + self.y_buf[step - 1, i].astype(F32)
             self.added[i] = total.astype(BF16)
 
+        if self.quad_refs:
+            quad_buf, _ = self.quad_refs
+            half, member = lax.div(self.ctx, self.plan.quad), lax.rem(self.ctx, self.plan.quad)
+            for copy in self.quad_copies():
+                copy.start()
+            for j, side in enumerate((half, 1 - half)):
+                quad_buf[pl.ds(member, 1), j] = self.added[pl.ds(side * self.plan.quad + member, 1)]
+            return
         for copy in self.owner_copies():
             copy.start()
         self.dst[pl.ds(self.ctx, 1)] = self.added[pl.ds(self.ctx, 1)]
 
+    def quad_copies(self):
+        quad_buf, _ = self.quad_refs
+        half, member = lax.div(self.ctx, self.plan.quad), lax.rem(self.ctx, self.plan.quad)
+        copies = []
+        for i, (peer, to) in enumerate(quad_members(self.plan, half, member)):
+            for j, side in enumerate((half, 1 - half)):
+                copies.append(
+                    remote(
+                        self.added.at[side * self.plan.quad + to],
+                        quad_buf.at[member, j],
+                        self.send.at[2 * i + j],
+                        self.recv.at[2 * i + j],
+                        (self.dp, peer),
+                    )
+                )
+        return copies
+
+    def far_copy(self):
+        last = 2 * (self.plan.quad - 1)
+        far = lax.rem(self.ctx + self.plan.quad, self.plan.ctx)
+        away = self.quad_refs[1]
+        return remote(away, self.dst.at[1], self.send.at[last], self.recv.at[last], (self.dp, far))
+
+    def across(self):
+        quad_buf, away = self.quad_refs
+        for copy in self.quad_copies():
+            copy.wait()
+        for j in range(2):
+            total = quad_buf[0, j].astype(F32)
+            for i in range(1, self.plan.quad):
+                total = total + quad_buf[i, j].astype(F32)
+            if j == 0:
+                self.dst[0] = total.astype(BF16)
+            else:
+                away[...] = total.astype(BF16)
+        self.far_copy().start()
+
     def finish(self):
+        if self.quad_refs:
+            self.far_copy().wait()
+            return
         for copy in self.owner_copies():
             copy.wait()
 
@@ -1032,7 +1081,7 @@
             for step in range(1, plan.quad)
         ]
     )
-    fold_refs, out_refs = refs[:18], refs[18:]
+    fold_refs, out_refs = refs[:20], refs[20:]
     out_sum = None
     if not summed:
         grid = Grid(plan)
@@ -1056,9 +1105,8 @@
             )
             copy.start()
             arriving.append(copy)
-    count = len(fold_refs) // 2
-    mix_fold = Fold(plan, dwo, rwo, *fold_refs[:3], fold_refs[3:count])
-    qkv_fold = Fold(plan, dwq, rwq, *fold_refs[count : count + 3], fold_refs[count + 3 :])
+    mix_fold = Fold(plan, dwo, rwo, *fold_refs[:3], fold_refs[3:9], fold_refs[9:11])
+    qkv_fold = Fold(plan, dwq, rwq, *fold_refs[11:14], fold_refs[14:20])
     if plan.tiled:
         for i in range(plan.quad):
             part = tn(mixed[i].reshape(plan.local, plan.head_cols), attn_grad)
@@ -1194,7 +1242,9 @@
         value = padded_rows(plan, value, plan.devices).astype(BF16)
         dwq[:, :, :, cols] = value.reshape(plan.dp, plan.ctx, plan.pad_rows, 128)
 
+    mix_fold.across()
     qkv_fold.start()
+    qkv_fold.along_y()
     local, width = plan.local, plan.width
     if out_sum:
         out_sum.phase(2)
@@ -1237,7 +1287,6 @@
 
     swap_grad = remote(grad_away, grad_out.at[half], s_send.at[1], s_recv.at[1], across)
     swap_grad.start()
-    qkv_fold.along_y()
     if out_sum:
         out_sum.phase(3)
     branches = out_sum.work.at[0] if out_sum else out_part
@@ -1304,7 +1353,7 @@
         functools.partial(back_kernel, plan, summed),
         out_shape=(
             jax.ShapeDtypeStruct((plan.ctx, plan.pad_rows, plan.wide), BF16),
-            jax.ShapeDtypeStruct((plan.ctx, plan.rows, width), BF16),
+            jax.ShapeDtypeStruct((2, plan.rows, width), BF16),
             jax.ShapeDtypeStruct(dealt, BF16),
             jax.ShapeDtypeStruct((plan.branches, plan.own_hidden, width), BF16),
             jax.ShapeDtypeStruct((2, block, width), BF16),
@@ -1340,6 +1389,10 @@
             DMA((3,)),
         ]
         + fold_scratch(plan, plan.rows, width)
+        + [
+            pltpu.VMEM((plan.quad, 2, plan.rows, width), BF16),
+            pltpu.VMEM((plan.rows, width), BF16),
+        ]
         + fold_scratch(plan, plan.pad_rows, plan.wide)
         + ([] if summed else out_scratch),
         compiler_params=params(collective_id),
@@ -1832,10 +1885,7 @@
     gain_one[...] = columns[64:72, :rows][:1]
     gain_two[...] = columns[64:72, :rows][1:2]
     router[...] = total[:, 66 : 66 + plan.experts]
-    mixed = r_mix[0].astype(F32)
-    for i in range(1, plan.ctx):
-        mixed = mixed + r_mix[i].astype(F32)
-    attn_out[...] = mixed
+    attn_out[...] = r_mix[0].astype(F32) + r_mix[1].astype(F32)
     half = lax.div(lax.axis_index("ctx"), plan.quad)
     for branch in range(plan.branches):
         value = dw_out[branch, pl.ds(half, 1)][0] + far_out[branch].astype(F32)

time: 327 us -> 327 us (level)
  no operation moved by 1% of the time
where the time goes in v2:
time: 327 us; the launch traced here: 326 us
  Pallas kernels  310 us (95%)
  other arithmetic  5.93 us (2%)
  local copies, waits for them, and re-layouts  5.37 us (2%)
  starting transfers between devices  4.1 us (1%)
    pallas_call x1, Pallas kernels, back(): pl.pallas_call(functools.partial(back_kernel, plan, summed), out_shape=(j...  113 us
    pallas_call x1, Pallas kernels, front(): pl.pallas_call(functools.partial(front_kernel, plan), out_shape=(jax.Shap...  105 us
    pallas_call x1, Pallas kernels, fused(): pl.pallas_call(functools.partial(fused_kernel, plan), out_shape=(jax.Shap...  82.1 us
  transfers between devices with their start and end apart: 1, of which 0 were waited for; matrix products, arithmetic and copies ran while one was open for 2% of the time, Pallas kernels for 33%

profile of v2, /device:TPU:0, one launch (start us, length us, event | category | flops | bytes accessed | tf_op | source)
XLA Modules:
  0.0 326.3 jit_solution(136840862042277887)
XLA Ops:
  0.6 0.0 copy-start.7
  0.7 0.0 copy-start.8
  0.7 0.0 copy-start.10
  0.7 0.0 copy-start.11
  0.7 1.1 copy.52
  1.9 1.0 fusion.2
  2.8 4.1 %collective-permute-start = (bf16[5,64,768]{2,1,0:T(8,128)(2,1)S(1)}, bf16[5,64,768]{2,1,0:T(8,128)(2,1)S(1)}, u32[]{:S(2)}, u32[]{:S(2)}) collective-permute-start(bf16[5,64,768]{2,1,0:T(8,128)(2,1)S(1)} %get-tuple-element.119), channel_id=1, source_target_pairs={{0,4},{1,5},{2,6},{3,7},{4,0},{5,1},{6,2},{7,3},{8,12},{9,13},{10,... | collective-permute-start | bytes 1474568 | tf_op jit(solution)/shard_map/ppermute | solution.py:2028
  7.0 0.1 copy.50
  7.1 0.4 copy.58
  7.5 0.0 copy-done.12
  7.5 0.6 constant_dynamic-slice_fusion
  8.1 0.1 compare_convert_fusion
  8.2 0.7 pad.8.extra
  8.9 0.1 bitcast_multiply_fusion.1
  9.0 0.0 copy-start.3
  9.0 0.0 copy-start.4
  9.0 0.0 copy-start.5
  9.0 0.0 copy-start.6
  9.0 2.0 pad_maximum_fusion.both
  11.0 0.8 fusion.1.gyw
  11.9 3.2 pack.1
  15.0 0.0 copy-done.4
  15.0 0.9 multiply_add_fusion
  16.0 0.9 bitcast_multiply_fusion.sine
  16.8 105.2 %front.1 = (bf16[8,128,768]{2,1,0:T(8,128)(2,1)}, bf16[768,640]{1,0:T(8,128)(2,1)}, bf16[1024,768]{1,0:T(8,128)(2,1)}, bf16[1024,384]{1,0:T(8,128)(2,1)}, bf16[1...) custom-call(s32[1]{0:T(128)} %bitcast.length_ref, ...), custom_call_target="tpu_custom_call" | custom-call | bytes 306000000 | tf_op jit(solution)/shard_map/front/pallas_call | solution.py:763
  122.1 0.0 collective-permute-done
  122.1 0.2 maximum_select_fusion
  122.2 1.0 copy.53
  123.3 82.1 %fused.1 = (f32[272,768]{1,0:T(8,128)}, bf16[768,1280]{1,0:T(8,128)(2,1)}, f32[640,768]{1,0:T(8,128)}, bf16[16,256,768]{2,1,0:T(8,128)(2,1)}) custom-call(bf16[272,768]{1,0:T(8,128)(2,1)} %get-tuple-element.56.n2x.rest_2_, bf16[16,2,160,768]{3,2,1,0:T(8,128)(2,1)} %get-tuple-element.57.gy, bf16[768,1280]{1,0:T(8,128)(2,1)} %get-tuple-element.58.w_in, ...), custom_call_target="tpu_custom_call" | custom-call | bytes 340000000 | tf_op jit(solution)/shard_map/fused/pallas_call | solution.py:1740
  205.4 113.3 %back.1 = (bf16[8,24,640]{2,1,0:T(8,128)(2,1)}, bf16[2,24,768]{2,1,0:T(8,128)(2,1)}, bf16[16,48,640]{2,1,0:T(8,128)(2,1)}, bf16[5,64,768]{2,1,0:T(8,128)(2,1)}, ...) custom-call(s32[1]{0:T(128)} %bitcast.length_ref, bf16[1024,768]{1,0:T(8,128)(2,1)} %bitcast.48, ...), custom_call_target="tpu_custom_call" | custom-call | bytes 306000000 | tf_op jit(solution)/shard_map/back/pallas_call | solution.py:1352
  318.6 6.3 %unpack.1 = (f32[24,4096]{1,0:T(8,128)}, f32[24,4,4096]{2,1,0:T(4,128)}, f32[24,2304]{1,0:T(8,128)}, f32[24,768]{1,0:T(8,128)}, f32[1,24]{1,0:T(1,128)}, /*index...) custom-call(bf16[16,48,640]{2,1,0:T(8,128)(2,1)} %get-tuple-element., ...), custom_call_target="tpu_custom_call" | custom-call | bytes 17000000 | tf_op jit(solution)/shard_map/unpack/pallas_call | solution.py:1900
  324.9 1.4 copy.56
  (20 shorter events, 0.1 us)
Async XLA Ops:
  0.6 6.3 %copy-start.7 = (s32[2,1,128,2]{2,3,1,0:T(2,128)S(1)}, s32[2,1,128,2]{2,3,1,0:T(2,128)}, u32[]{:S(2)}) copy-start(s32[2,1,128,2]{2,3,1,0:T(2,128)} %param.21) | copy-start | bytes 6148
  0.7 6.3 %copy-start.8 = (bf16[24,4]{0,1:T(4,128)(2,1)S(1)}, bf16[24,4]{0,1:T(4,128)(2,1)}, u32[]{:S(2)}) copy-start(bf16[24,4]{0,1:T(4,128)(2,1)} %param.27) | copy-start | bytes 580
  0.7 6.3 %copy-start.10 = (bf16[24]{0:T(256)(128)(2,1)S(1)}, bf16[24]{0:T(256)(128)(2,1)}, u32[]{:S(2)}) copy-start(bf16[24]{0:T(256)(128)(2,1)} %param.26) | copy-start | bytes 148
  0.7 6.3 %copy-start.11 = (bf16[24]{0:T(256)(128)(2,1)S(1)}, bf16[24]{0:T(256)(128)(2,1)}, u32[]{:S(2)}) copy-start(bf16[24]{0:T(256)(128)(2,1)} %param.23) | copy-start | bytes 148
  0.7 6.4 %copy-start = (bf16[24,4,4096]{2,1,0:T(4,128)(2,1)S(1)}, bf16[24,4,4096]{2,1,0:T(4,128)(2,1)}, u32[]{:S(2)}) copy-start(bf16[24,4,4096]{2,1,0:T(4,128)(2,1)} %param.30) | copy-start | bytes 2359300
  0.7 6.8 %copy-start.12 = (s32[2,1]{0,1:T(1,128)S(1)}, s32[2,1]{0,1:T(1,128)}, u32[]{:S(2)}) copy-start(s32[2,1]{0,1:T(1,128)} %param.20) | copy-start | bytes 28
  0.7 8.2 %copy-start.1 = (bf16[2,1,128,768]{3,2,1,0:T(8,128)(2,1)S(1)}, bf16[2,1,128,768]{3,2,1,0:T(8,128)(2,1)}, u32[]{:S(2)}) copy-start(bf16[2,1,128,768]{3,2,1,0:T(8,128)(2,1)} %param.22) | copy-start | bytes 1179652
  2.8 119.2 %collective-permute-start = (bf16[5,64,768]{2,1,0:T(8,128)(2,1)S(1)}, bf16[5,64,768]{2,1,0:T(8,128)(2,1)S(1)}, u32[]{:S(2)}, u32[]{:S(2)}) collective-permute-start(bf16[5,64,768]{2,1,0:T(8,128)(2,1)S(1)} %get-tuple-element.119), channel_id=1, source_target_pairs={{0,4},{1,5},{2,6},{3,7},{4,0},{5,1},{6,2},{7,3},{8,12},{9,13},{10,... | collective-permute-start | bytes 1474568 | tf_op jit(solution)/shard_map/ppermute | solution.py:2028
  7.1 3.9 %copy-start.2 = (bf16[24,768]{1,0:T(8,128)(2,1)S(1)}, bf16[24,768]{1,0:T(8,128)(2,1)}, u32[]{:S(2)}) copy-start(bf16[24,768]{1,0:T(8,128)(2,1)} %param.25) | copy-start | bytes 110596
  9.0 6.1 %copy-start.3 = (f32[64,128]{1,0:T(8,128)S(1)}, f32[64,128]{1,0:T(8,128)}, u32[]{:S(2)}) copy-start(f32[64,128]{1,0:T(8,128)} %constant.33.clone) | copy-start | bytes 98308
  9.0 6.0 %copy-start.4 = (f32[64,128]{1,0:T(8,128)S(1)}, f32[64,128]{1,0:T(8,128)}, u32[]{:S(2)}) copy-start(f32[64,128]{1,0:T(8,128)} %constant.32.clone) | copy-start | bytes 98308
  9.0 6.0 %copy-start.5 = (f32[16,128]{1,0:T(8,128)S(1)}, f32[16,128]{1,0:T(8,128)}, u32[]{:S(2)}) copy-start(f32[16,128]{1,0:T(8,128)} %constant.31.clone) | copy-start | bytes 24580
  9.0 6.0 %copy-start.6 = (f32[16,128]{1,0:T(8,128)S(1)}, f32[16,128]{1,0:T(8,128)}, u32[]{:S(2)}) copy-start(f32[16,128]{1,0:T(8,128)} %constant.30.clone) | copy-start | bytes 24580
  11.0 5.0 %copy-start.9 = (f32[128]{0:T(128)S(1)}, f32[128]{0:T(128)}, u32[]{:S(2)}) copy-start(f32[128]{0:T(128)} %constant.51) | copy-start | bytes 1540
